TPU v7x, 256 devices: a whole 4x4x8 slice. The times are simulated.
256 devices in a mesh: cls: 4 (over y), dom: 64 (over z, x, core).
Axes of the slice: x: 4, y: 4, z: 8, core: 2. Of those that a mesh axis runs over, the one named last changes fastest.
Arguments:
- particles: bfloat16 [65536, 4096], P('dom', 'cls'), may hold values from -6 to 8
- candidates: int32 [65536, 2], P('dom'), may hold values from 0 to 63, all different within a row; in each aligned block of 1024 rows (0 to 1023, 1024 to 2047, ...) at most 64 rows name the same one
- defocus: int32 [65536], P('dom'), may hold values from 0 to 31
- ctf_table: float32 [32, 4096], P(None, 'cls'), may hold values from -1 to 1
- references: bfloat16 [256, 4096], P('dom', 'cls'), may hold values from -5 to 5
- rotations: bfloat16 [64, 64, 64], replicated, may hold values from -0.4 to 1.1
Outputs:
- class_sums: bfloat16 [256, 4096], P('dom', 'cls')
- class_weights: float32 [256, 4096], P('dom', 'cls')
- log_evidence: float32 [65536], P('dom')
Inputs may be any that keep to these rules, and one draw needn't show every extreme that they name: The two candidates of a particle differ; among the 1024 particles of one index of dom no group is named by more than 64 entries, a bound that some block reaches.
All inputs are finite; a program needn't handle non-finite values.
Results may differ from a plain program's by a relative error of at most 0.0054.
Values may be sent and summed in bfloat16 or wider, within the bound.
A program may use at most 128 MiB of HBM per device.

v0:
```python
import math

import jax
import jax.numpy as jnp
from jax import lax
from jax.sharding import PartitionSpec as P

highest = lax.Precision.HIGHEST


def sent_together(arrays, axis, split_dim, concat_dim, along):
    widths = [a.shape[along] for a in arrays]
    both = jnp.concatenate(arrays, axis=along)
    out = lax.all_to_all(both, axis, split_axis=split_dim, concat_axis=concat_dim, tiled=True)
    return tuple(jnp.split(out, [sum(widths[:k]) for k in range(1, len(widths))], axis=along))


def split_up(shard, dim, peers):
    before, after = (shard.shape[:dim], shard.shape[dim + 1 :])
    return jnp.moveaxis(shard.reshape(*before, peers, -1, *after), dim, 0)


def summed_on_arrival(shard, axis, dim):
    peers = lax.axis_size(axis)
    parts = lax.all_to_all(split_up(shard, dim, peers), axis, 0, 0, tiled=True)
    return jnp.sum(parts, axis=0)


def turned_gather(arrays, axis, dims):
    turned = [jnp.moveaxis(a, dim, 0) for a, dim in zip(arrays, dims)]
    both = jnp.concatenate([t.reshape(len(t), -1) for t in turned], axis=1)
    out, at, finished = (lax.all_gather(both, axis, axis=0, tiled=True), 0, [])
    for t, dim in zip(turned, dims):
        piece = out[:, at : at + t[0].size].reshape(-1, *t.shape[1:])
        finished.append(jnp.moveaxis(piece, 0, dim))
        at += t[0].size
    return tuple(finished)


def joined_along(parts, dim):
    parts = jnp.moveaxis(parts, 0, dim)
    shape = parts.shape
    return parts.reshape(*shape[:dim], shape[dim] * shape[dim + 1], *shape[dim + 2 :])


def from_everyone(shard, axis):
    peers = lax.axis_size(axis)
    return lax.all_to_all(
        jnp.broadcast_to(shard[None], (peers, *shard.shape)), axis, 0, 0, tiled=True
    )


def gathered_copies(shard, axis, dim):
    return joined_along(from_everyone(shard, axis), dim)


def route_slots(candidates, owners):
    entries = candidates.reshape(-1)
    owner_ids = lax.broadcasted_iota(jnp.int32, (entries.shape[0], owners), 1)
    onehot_owner = (entries[:, None] == owner_ids).astype(jnp.int32)
    entry_rank = jnp.cumsum(onehot_owner, axis=0) - onehot_owner
    slot_of = jnp.sum(entry_rank * onehot_owner, axis=1)
    return (entries, slot_of)


def local(particles, candidates, defocus, ctf_table, references, rotations):
    local_count, pixel_share = particles.shape
    owners = lax.axis_size("dom")
    capacity = 4 * local_count // owners
    slot_count = owners * capacity
    entries, slot_of = route_slots(candidates, owners)
    entry_ids = jnp.arange(entries.shape[0], dtype=jnp.int32)
    slot_entry = jnp.full((owners, capacity), -1, jnp.int32).at[entries, slot_of].set(entry_ids)
    send_live = slot_entry >= 0
    send_rows = jnp.maximum(slot_entry, 0) // 2
    send_pixels = jnp.where(
        send_live[:, :, None], particles[send_rows], jnp.zeros((), jnp.bfloat16)
    )
    send_defocus = jnp.where(send_live, defocus[send_rows], -1)
    arrived, arrived_defocus = (
        lax.all_to_all(send_pixels, "dom", split_axis=0, concat_axis=0, tiled=True),
        lax.all_to_all(send_defocus, "dom", split_axis=0, concat_axis=0, tiled=True),
    )
    defocus_kinds = ctf_table.shape[0]
    class_count = references.shape[0]
    turn_count = rotations.shape[0]
    angles = rotations.shape[1]
    cycle_share = pixel_share // angles
    pair_count = class_count * turn_count
    flat_defocus = arrived_defocus.reshape(slot_count)
    owner_live = flat_defocus >= 0
    kind_ids = lax.broadcasted_iota(jnp.int32, (slot_count, defocus_kinds), 1)
    picked = (flat_defocus[:, None] == kind_ids).astype(jnp.float32)
    rotated = jnp.einsum(
        "cla,rba->crlb",
        references.reshape(class_count, cycle_share, angles),
        rotations,
        preferred_element_type=jnp.float32,
    )
    rotated = rotated.astype(jnp.bfloat16).reshape(pair_count, pixel_share)
    block_rows = min(512, slot_count)
    block_count = slot_count // block_rows

    def score_block(packed):
        pixel_rows, picked_rows = packed
        ctf_rows = jnp.dot(picked_rows, ctf_table, precision=highest)
        weighted = (pixel_rows.astype(jnp.float32) * ctf_rows).astype(jnp.bfloat16)
        cross_term = lax.dot_general(
            weighted, rotated, (((1,), (1,)), ((), ())), preferred_element_type=jnp.float32
        )
        return (weighted, cross_term)

    weighted, cross_term = lax.map(
        score_block,
        (
            arrived.reshape(block_count, block_rows, pixel_share),
            picked.reshape(block_count, block_rows, defocus_kinds),
        ),
    )
    weighted = weighted.reshape(slot_count, pixel_share)
    cross_term = cross_term.reshape(slot_count, pair_count)
    ctf_power = ctf_table * ctf_table
    square = rotated.astype(jnp.float32) ** 2
    energy = lax.dot_general(ctf_power, square, (((1,), (1,)), ((), ())), precision=highest)
    partial_value = cross_term - 0.5 * jnp.dot(picked, energy, precision=highest)
    inverse_noise = 4.0 / math.sqrt(pixel_share * lax.axis_size("cls"))
    score_share = inverse_noise * summed_on_arrival(partial_value, "cls", 0)
    share_rows = score_share.shape[0]
    share_max = jnp.max(score_share, axis=1)
    share_sum = jnp.sum(jnp.exp(score_share - share_max[:, None]), axis=1)
    slot_max, slot_sum = turned_gather((share_max, share_sum), "cls", (0, 0))
    back_max, back_sum = sent_together(
        (slot_max.reshape(owners, capacity), slot_sum.reshape(owners, capacity)), "dom", 0, 0, 1
    )
    pair_max = back_max[entries, slot_of].reshape(local_count, 2)
    pair_sum = back_sum[entries, slot_of].reshape(local_count, 2)
    pair_best = jnp.max(pair_max, axis=1, keepdims=True)
    log_evidence = pair_best[:, 0] + jnp.log(
        jnp.sum(pair_sum * jnp.exp(pair_max - pair_best), axis=1)
    )
    send_log = jnp.where(send_live, log_evidence[send_rows], 0.0)
    slot_log = lax.all_to_all(send_log, "dom", split_axis=0, concat_axis=0, tiled=True)
    log_evidence, slot_log = (log_evidence, slot_log.reshape(slot_count))
    offset = lax.axis_index("cls") * share_rows
    share_log = lax.dynamic_slice_in_dim(slot_log, offset, share_rows)
    share_live = lax.dynamic_slice_in_dim(owner_live, offset, share_rows)
    share_weights = jnp.where(
        share_live[:, None], jnp.exp(score_share - share_log[:, None]), 0.0
    ).astype(jnp.bfloat16)
    weights = gathered_copies(share_weights, "cls", 0)
    rot_sum = lax.dot_general(
        weights, weighted, (((0,), (0,)), ((), ())), preferred_element_type=jnp.float32
    )
    pair_kind = lax.dot_general(
        weights,
        picked.astype(jnp.bfloat16),
        (((0,), (0,)), ((), ())),
        preferred_element_type=jnp.float32,
    )
    rot_weight = jnp.dot(pair_kind, ctf_power, precision=highest)
    turn_maps = rotations.astype(jnp.float32)
    back_sum = jnp.einsum(
        "crlb,rba->cla",
        rot_sum.reshape(class_count, turn_count, cycle_share, angles),
        turn_maps,
        precision=highest,
    )
    back_weight = jnp.einsum(
        "crlb,rba->cla",
        rot_weight.reshape(class_count, turn_count, cycle_share, angles),
        turn_maps,
        precision=highest,
    )
    class_sums = back_sum.reshape(class_count, pixel_share).astype(jnp.bfloat16)
    class_weights = back_weight.reshape(class_count, pixel_share)
    return (class_sums, class_weights, log_evidence)


def solution(mesh):
    in_specs = (P("dom", "cls"), P("dom", None), P("dom"), P(None, "cls"), P("dom", "cls"), P())
    out_specs = (P("dom", "cls"), P("dom", "cls"), P("dom"))
    return jax.shard_map(local, mesh=mesh, in_specs=in_specs, out_specs=out_specs, check_vma=False)
```

profile of v0, /device:TPU:1, one launch (start us, length us, event | category | flops | bytes accessed | tf_op | source)
XLA Modules:
  0.0 526.8 jit_solution(7144400860387845022)
XLA Ops:
  2.6 18.1 %reduce-window.6 = s32[64,16,128]{2,1,0:T(8,128)S(1)} reduce-window(s32[64,16,128]{2,1,0:T(8,128)S(1)} %fusion.25, s32[]{:T(128)} %constant.26.clone.1), window={size=1x1x128 pad=0_0x0_0x127_0}, to_apply=%region_0.0 | reduce-window | flops 16646144 | bytes 1048580 | tf_op jit(solution)/shard_map/reduce-window
  22.3 8.1 %scatter_custom_fusion = s32[4096]{0:T(1024)S(1)} fusion(s32[2048]{0:T(1024)S(1)} %broadcast_select_fusion.3, s32[2048]{0:T(1024)S(1)} %iota.22, s32[]{:T(128)} %constant.23.clone.1), kind=kCustom, calls=%fused_computation.72 | custom fusion | bytes 16388
  30.7 16.7 %gather_fusion = s32[4096]{0:T(1024)S(1)} fusion(s32[1024]{0:T(1024)S(1)} %copy-done.3, s32[4096]{0:T(1024)S(1)} %broadcast_clamp_fusion), kind=kCustom, calls=%fused_computation | custom fusion | bytes 49152 | tf_op jit(solution)/shard_map/gather | solution.py:79
  48.1 13.0 %all-to-all-start = ((s32[64,1,64]{2,1,0:T(1,128)}), s32[64,1,64]{2,1,0:T(1,128)S(1)}, u32[]{:S(2)}, u32[]{:S(2)}) async-start(s32[64,1,64]{2,1,0:T(1,128)} %bitcast.8), calls=%async_computation | async-start | bytes 65536 | tf_op jit(solution)/shard_map/all_to_all | solution.py:82
  61.1 18.3 %gather_fusion.1 = bf16[4096,1024]{1,0:T(8,128)(2,1)} fusion(bf16[1024,1024]{1,0:T(8,128)(2,1)S(1)} %copy-done, s32[4096]{0:T(1024)S(1)} %broadcast_clamp_fusion), kind=kCustom, calls=%fused_computation.1 | custom fusion | bytes 16793600 | tf_op jit(solution)/shard_map/gather | solution.py:77
  79.4 7.2 %broadcast_select_fusion = bf16[64,64,1024]{2,1,0:T(8,128)(2,1)} fusion(bf16[64,64,1024]{2,1,0:T(8,128)(2,1)} %bitcast.112, pred[64,64]{1,0:T(8,128)(4,1)S(1)} %reshape.189), kind=kLoop, calls=%fused_computation.14 | loop fusion | flops 4194304 | bytes 16781312 | tf_op jit(solution)/shard_map/jit(_where)/select_n | solution.py:76
  86.6 10.6 %all-to-all-start.1 = ((bf16[64,64,1024]{2,1,0:T(8,128)(2,1)}), bf16[64,64,1024]{2,1,0:T(8,128)(2,1)}, u32[]{:S(2)}, u32[]{:S(2)}) async-start(bf16[64,64,1024]{2,1,0:T(8,128)(2,1)} %broadcast_select_fusion), calls=%async_computation.1 | async-start | bytes 16777216 | tf_op jit(solution)/shard_map/all_to_all | solution.py:81
  103.5 176.1 %all-to-all-done.1 = bf16[64,64,1024]{2,1,0:T(8,128)(2,1)} async-done(((bf16[64,64,1024]{2,1,0:T(8,128)(2,1)}), bf16[64,64,1024]{2,1,0:T(8,128)(2,1)}, u32[]{:S(2)}, u32[]{:S(2)}) %all-to-all-start.1) | async-done | bytes 8388640 | tf_op jit(solution)/shard_map/all_to_all | solution.py:81
  279.6 43.4 %while.12 = (s32[]{:T(128)}, bf16[8,512,1024]{2,1,0:T(8,128)(2,1)}, f32[8,512,256]{2,1,0:T(8,128)}, bf16[8,512,1024]{2,1,0:T(8,128)(2,1)}, f32[8,512,32]{2,1,0:T...) while((s32[]{:T(128)}, bf16[8,512,1024]{2,1,0:T(8,128)(2,1)}, ...), condition=%wide.region_5.6_spmd, body=%wide.region_4.5_spmd.sunk | while | flops 471334912 | bytes 5637717 | solution.py:113
  285.0 4.2 bitcast_dynamic-update-slice_fusion.2
  306.7 4.1 bitcast_dynamic-update-slice_fusion.2
  312.2 4.1 bitcast_dynamic-update-slice_fusion.2
  327.0 48.4 %all_to_all.45 = f32[4,1024,256]{2,1,0:T(8,128)} all-to-all(f32[4,1024,256]{2,1,0:T(8,128)S(1)} %bitcast.113), channel_id=1, replica_groups=mesh['cls'=4,'dom'=64] {'cls'}, dimensions={0} | all-to-all | bytes 8388608 | tf_op jit(solution)/shard_map/all_to_all | solution.py:25
  378.7 9.0 %all_gather.3 = f32[4096,2]{0,1:T(2,128)S(1)} all-gather(f32[1024,2]{0,1:T(2,128)S(1)} %pad_maximum_fusion.1), channel_id=1, replica_groups=mesh['cls'=4,'dom'=64] {'cls'}, dimensions={0}, use_global_device_ids=true | all-gather | bytes 40960 | tf_op jit(solution)/shard_map/all_gather | solution.py:32
  388.6 17.8 %all-to-all-start.3 = ((f32[64,1,128]{2,1,0:T(1,128)}), f32[64,1,128]{2,1,0:T(1,128)S(1)}, u32[]{:S(2)}, u32[]{:S(2)}) async-start(f32[64,1,128]{2,1,0:T(1,128)} %bitcast.19), calls=%async_computation.3 | async-start | bytes 65536 | tf_op jit(solution)/shard_map/all_to_all | solution.py:14
  406.5 9.4 %all-to-all-done.3 = f32[64,1,128]{2,1,0:T(1,128)S(1)} async-done(((f32[64,1,128]{2,1,0:T(1,128)}), f32[64,1,128]{2,1,0:T(1,128)S(1)}, u32[]{:S(2)}, u32[]{:S(2)}) %all-to-all-start.3) | async-done | bytes 32800 | tf_op jit(solution)/shard_map/all_to_all | solution.py:14
  415.9 13.6 %gather_fusion.3 = f32[2048]{0:T(1024)S(1)} fusion(f32[64,64]{1,0:T(8,128)S(1)} %get-tuple-element.61, s32[2048]{0:T(1024)S(1)} %bitcast.110), kind=kCustom, calls=%fused_computation.3 | custom fusion | bytes 32768 | tf_op jit(solution)/shard_map/gather | solution.py:136
  430.0 13.6 %gather_fusion.2 = f32[2048]{0:T(1024)S(1)} fusion(f32[64,64]{1,0:T(8,128)S(1)} %get-tuple-element.62, s32[2048]{0:T(1024)S(1)} %bitcast.111), kind=kCustom, calls=%fused_computation.2 | custom fusion | bytes 32768 | tf_op jit(solution)/shard_map/gather | solution.py:135
  444.7 16.7 %gather_fusion.4 = f32[4096]{0:T(1024)S(1)} fusion(f32[1024]{0:T(1024)S(1)} %log_add_fusion, s32[4096]{0:T(1024)S(1)} %broadcast_clamp_fusion), kind=kCustom, calls=%fused_computation.4 | custom fusion | bytes 49152 | tf_op jit(solution)/shard_map/gather | solution.py:141
  462.1 4.7 all-to-all-start.4
  466.9 9.5 %all-to-all-done.4 = f32[64,1,64]{2,1,0:T(1,128)S(1)} async-done(((f32[64,1,64]{2,1,0:T(1,128)}), f32[64,1,64]{2,1,0:T(1,128)S(1)}, u32[]{:S(2)}, u32[]{:S(2)}) %all-to-all-start.4) | async-done | bytes 16416 | tf_op jit(solution)/shard_map/all_to_all | solution.py:142
  483.5 11.3 %copy.52 = bf16[4096,1024]{0,1:T(8,128)(2,1)} copy(bf16[4096,1024]{1,0:T(8,128)(2,1)} %bitcast.114) | data formatting | bytes 16777216 | tf_op jit(solution)/shard_map/reshape | solution.py:120
  494.8 14.5 %all-to-all-done.5 = bf16[4,1024,256]{1,2,0:T(8,128)(2,1)S(1)} async-done(((bf16[4,1024,256]{1,2,0:T(8,128)(2,1)}), bf16[4,1024,256]{1,2,0:T(8,128)(2,1)S(1)}, u32[]{:S(2)}, u32[]{:S(2)}) %all-to-all-start.5) | async-done | bytes 2097184 | tf_op jit(solution)/shard_map/all_to_all | solution.py:48
  516.2 7.7 %fusion.36 = f32[4,64,16,64]{3,1,2,0:T(8,128)S(1)} fusion(bf16[4,64,4096,1]{2,1,3,0:T(8,128)(2,1)} %bitcast.118, bf16[16,64,4096,1]{2,1,0,3:T(8,128)(2,1)} %bitcast.115), kind=kOutput, calls=%fused_computation.78 | convolution fusion | flops 2147483648 | bytes 11534336 | tf_op jit(solution)/shard_map/dot_general | solution.py:151
  (103 shorter events, 69.0 us)
Async XLA Ops:
  0.6 60.5 %copy-start = (bf16[1024,1024]{1,0:T(8,128)(2,1)S(1)}, bf16[1024,1024]{1,0:T(8,128)(2,1)}, u32[]{:S(2)}) copy-start(bf16[1024,1024]{1,0:T(8,128)(2,1)} %param.8) | copy-start | bytes 6291460
  0.6 21.5 %copy-start.8 = (s32[2]{0:T(128)S(1)}, s32[2]{0:T(128)}, u32[]{:S(2)}) copy-start(s32[2]{0:T(128)} %constant.65) | copy-start | bytes 28
  0.7 30.0 %copy-start.3 = (s32[1024]{0:T(1024)S(1)}, s32[1024]{0:T(1024)}, u32[]{:S(2)}) copy-start(s32[1024]{0:T(1024)} %param.10) | copy-start | bytes 12292
  48.1 38.5 %all-to-all-start = ((s32[64,1,64]{2,1,0:T(1,128)}), s32[64,1,64]{2,1,0:T(1,128)S(1)}, u32[]{:S(2)}, u32[]{:S(2)}) async-start(s32[64,1,64]{2,1,0:T(1,128)} %bitcast.8), calls=%async_computation | async-start | bytes 65536 | tf_op jit(solution)/shard_map/all_to_all | solution.py:82
  86.6 10.7 %copy-start.7 = (bf16[4,1024]{1,0:T(4,128)(2,1)S(1)}, bf16[4,1024]{1,0:T(4,128)(2,1)}, u32[]{:S(2)}) copy-start(bf16[4,1024]{1,0:T(4,128)(2,1)} %param.12) | copy-start | bytes 24580
  86.6 10.8 %copy-start.4 = (bf16[64,64,64]{2,1,0:T(8,128)(2,1)S(1)}, bf16[64,64,64]{2,1,0:T(8,128)(2,1)}, u32[]{:S(2)}) copy-start(bf16[64,64,64]{2,1,0:T(8,128)(2,1)} %param.13) | copy-start | bytes 1572868
  86.6 193.0 %all-to-all-start.1 = ((bf16[64,64,1024]{2,1,0:T(8,128)(2,1)}), bf16[64,64,1024]{2,1,0:T(8,128)(2,1)}, u32[]{:S(2)}, u32[]{:S(2)}) async-start(bf16[64,64,1024]{2,1,0:T(8,128)(2,1)} %broadcast_select_fusion), calls=%async_computation.1 | async-start | bytes 16777216 | tf_op jit(solution)/shard_map/all_to_all | solution.py:81
  97.2 2.2 copy-start.6
  388.6 27.3 %all-to-all-start.3 = ((f32[64,1,128]{2,1,0:T(1,128)}), f32[64,1,128]{2,1,0:T(1,128)S(1)}, u32[]{:S(2)}, u32[]{:S(2)}) async-start(f32[64,1,128]{2,1,0:T(1,128)} %bitcast.19), calls=%async_computation.3 | async-start | bytes 65536 | tf_op jit(solution)/shard_map/all_to_all | solution.py:14
  444.7 16.7 %copy-start.2 = (f32[1024]{0:T(1024)}, f32[1024]{0:T(1024)S(1)}, u32[]{:S(2)}) copy-start(f32[1024]{0:T(1024)S(1)} %log_add_fusion) | copy-start | bytes 12292
  462.1 14.2 %all-to-all-start.4 = ((f32[64,1,64]{2,1,0:T(1,128)}), f32[64,1,64]{2,1,0:T(1,128)S(1)}, u32[]{:S(2)}, u32[]{:S(2)}) async-start(f32[64,1,64]{2,1,0:T(1,128)} %bitcast.23), calls=%async_computation.4 | async-start | bytes 65536 | tf_op jit(solution)/shard_map/all_to_all | solution.py:142
  479.9 29.4 %all-to-all-start.5 = ((bf16[4,1024,256]{1,2,0:T(8,128)(2,1)}), bf16[4,1024,256]{1,2,0:T(8,128)(2,1)S(1)}, u32[]{:S(2)}, u32[]{:S(2)}) async-start(bf16[4,1024,256]{1,2,0:T(8,128)(2,1)} %broadcast_in_dim.78), calls=%async_computation.5 | async-start | bytes 4194304 | tf_op jit(solution)/shard_map/all_to_all | solution.py:48
  509.4 1.4 copy-start.5
  516.2 10.6 %copy-start.1 = (bf16[1024,1024]{1,0:T(8,128)(2,1)S(1)}, bf16[1024,1024]{1,0:T(8,128)(2,1)}, u32[]{:S(2)}) copy-start(bf16[1024,1024]{1,0:T(8,128)(2,1)} %param.8) | copy-start | bytes 6291460
where the time goes:
time: 528 us; the launch traced here: 527 us
  waiting for transfers between devices  209 us (40%)
  local copies, waits for them, and re-layouts  110 us (21%)
  matrix products  63.2 us (12%)
  blocking collectives  57.4 us (11%)
  starting transfers between devices  49.8 us (9%)
  other arithmetic  35.5 us (7%)
    all_to_all x1, waiting for transfers between devices, local(): lax.all_to_all(send_pixels, 'dom', split_axis=0, concat_axis=0, tiled=True)  176 us
    all_to_all x1, blocking collectives, summed_on_arrival(): parts = lax.all_to_all(split_up(shard, dim, peers), axis, 0, 0, tiled=True)  48.4 us
    dot_general x8, matrix products, score_block(): ctf_rows = jnp.dot(picked_rows, ctf_table, precision=highest)  33 us
    another operation x3, other arithmetic  18.5 us
    gather x1, local copies, waits for them, and re-layouts, local(): particles[send_rows]  18.3 us
    all_to_all x1, starting transfers between devices, sent_together(): lax.all_to_all(both, axis, split_axis=split_dim, concat_axis=concat_dim,...  17.8 us
    gather x2, local copies, waits for them, and re-layouts, local(): send_log = jnp.where(send_live, log_evidence[send_rows], 0.0)  16.8 us
    gather x2, local copies, waits for them, and re-layouts, local(): send_defocus = jnp.where(send_live, defocus[send_rows], -1)  16.8 us
  transfers between devices with their start and end apart: 5, of which 4 were waited for; matrix products, arithmetic and copies ran while one was open for 8% of the time, Pallas kernels for 0%

commit v1 on v0

v1 whole, which is shorter than its diff:
```python
import functools

import jax
import jax.numpy as jnp
from jax import lax
from jax.experimental import pallas as pl
from jax.experimental.pallas import tpu as pltpu
from jax.sharding import PartitionSpec as P

F32 = jnp.float32
BF16 = jnp.bfloat16
I32 = jnp.int32
MESH = pl.DeviceIdType.MESH
NT = (((1,), (1,)), ((), ()))
NN = (((1,), (0,)), ((), ()))

GROUPS = 64
SLOTS = 64
ANG = 64
CYC = 16
CPG = 4
ROT = 64
PAIRS = CPG * ROT
PIX = CYC * ANG
KINDS = 32
TOK = 1024
SHARES = 4
ROWS = 640
PACKED = SHARES * ROWS
HI = ROWS // 64
VMEM_LIMIT = 60 * 1024 * 1024


def mm(a, b, dims=NN):
    return lax.dot_general(a, b, dims, preferred_element_type=F32)


def iota(shape, dim):
    return lax.broadcasted_iota(I32, shape, dim)


def pieces(x):
    p1 = x.astype(BF16)
    r1 = x - p1.astype(F32)
    p2 = r1.astype(BF16)
    p3 = (r1 - p2.astype(F32)).astype(BF16)
    return p1, p2, p3


def onehot(mask):
    return jnp.where(mask, 1.0, 0.0).astype(BF16)


def vm(n):
    return [pl.BlockSpec(memory_space=pltpu.VMEM)] * n


def route(cand_ref, kind_ref, tab_ref, kinds_ref, rho_ref):
    g_iota = iota((GROUPS, TOK), 0)
    tri = onehot(iota((256, 256), 0) < iota((256, 256), 1))
    count = jnp.zeros((GROUPS, 1), F32)
    owners, ranks = [], []
    for j in range(2):
        owner = onehot(g_iota == cand_ref[j : j + 1, :])
        owners.append(owner)
        row = []
        for blk in range(TOK // 256):
            part = owner[:, blk * 256 : (blk + 1) * 256]
            before = mm(part, tri) + count
            row.append(jnp.sum(before * part.astype(F32), axis=0, keepdims=True))
            count = count + jnp.sum(part.astype(F32), axis=1, keepdims=True)
        ranks.append(jnp.concatenate(row, axis=1))
    padded = jnp.floor((count + 7.0) * 0.125) * 8.0
    low = onehot(iota((GROUPS, GROUPS), 1) < iota((GROUPS, GROUPS), 0))
    offset = mm(low, jnp.broadcast_to(padded, (GROUPS, 128)).astype(BF16))[:, 0:1]
    tok = iota((1, TOK), 1)
    s_iota = iota((SLOTS, TOK), 0)
    high = jnp.zeros((GROUPS, SLOTS), F32)
    low_part = jnp.zeros((GROUPS, SLOTS), F32)
    for j in range(2):
        slot = onehot(s_iota == ranks[j].astype(I32))
        v1 = (tok // 8).astype(F32)
        v2 = ((tok % 8) * 32 + kind_ref[...]).astype(F32)
        high = high + mm(owners[j], (slot.astype(F32) * v1).astype(BF16), NT)
        low_part = low_part + mm(owners[j], (slot.astype(F32) * v2).astype(BF16), NT)
        at = jnp.sum(owners[j].astype(F32) * offset, axis=0, keepdims=True) + ranks[j]
        rho_ref[j : j + 1, :] = at.astype(I32)
    low_int = low_part.astype(I32)
    kinds = low_int % 32
    token = high.astype(I32) * 8 + low_int // 32
    s_lane = iota((GROUPS, SLOTS), 1)
    live = s_lane < count.astype(I32)
    tab_ref[:, 0:SLOTS] = token + 1024 * kinds
    extra = jnp.where(s_lane == 0, offset, jnp.where(s_lane == 1, count, padded))
    tab_ref[:, SLOTS : 2 * SLOTS] = extra.astype(I32)
    kinds_ref[:, 0:SLOTS] = jnp.where(live, kinds, -1)
    kinds_ref[:, SLOTS : 2 * SLOTS] = jnp.full((GROUPS, SLOTS), -1, I32)


def start_kernel(cand_ref, kind_ref, mine_ref, tab_ref, kinds_ref, rho_ref, all_ref, send_sem, recv_sem, own_sem):
    me = lax.axis_index("dom")
    row = lax.axis_index("cls")
    barrier = pltpu.get_barrier_semaphore()

    def greet(i, _):
        pl.semaphore_signal(barrier, inc=1, device_id=(row, lax.rem(me + i, GROUPS)), device_id_type=MESH)
        return 0

    lax.fori_loop(1, GROUPS, greet, 0)
    pl.semaphore_wait(barrier, GROUPS - 1)

    def copy(i):
        return pltpu.make_async_remote_copy(
            src_ref=mine_ref,
            dst_ref=all_ref.at[me],
            send_sem=send_sem.at[i],
            recv_sem=recv_sem.at[i],
            device_id=(row, lax.rem(me + i, GROUPS)),
            device_id_type=MESH,
        )

    def send(i, _):
        copy(i).start()
        return 0

    lax.fori_loop(1, GROUPS, send, 0)
    own = pltpu.make_async_copy(mine_ref, all_ref.at[me], own_sem)
    own.start()
    route(cand_ref, kind_ref, tab_ref, kinds_ref, rho_ref)
    own.wait()

    def finish(i, _):
        copy(i).wait()
        return 0

    lax.fori_loop(1, GROUPS, finish, 0)


def start_stage(cand_t, kinds_row, mine):
    return pl.pallas_call(
        start_kernel,
        out_shape=(
            jax.ShapeDtypeStruct((GROUPS, 2 * SLOTS), I32),
            jax.ShapeDtypeStruct((GROUPS, 2 * SLOTS), I32),
            jax.ShapeDtypeStruct((2, TOK), I32),
            jax.ShapeDtypeStruct((GROUPS, 32, 128), BF16),
        ),
        in_specs=vm(3),
        out_specs=tuple(vm(4)),
        scratch_shapes=[
            pltpu.SemaphoreType.DMA((GROUPS,)),
            pltpu.SemaphoreType.DMA((GROUPS,)),
            pltpu.SemaphoreType.DMA,
        ],
        compiler_params=pltpu.CompilerParams(collective_id=0, has_side_effects=True, vmem_limit_bytes=VMEM_LIMIT),
        name="start_stage",
    )(cand_t, kinds_row, mine)


def score_kernel(tab_ref, part_ref, refs_ref, rotq_ref, ctf_ref, kinds_ref, out_ref, wout_ref, xs, cs, spread, power, perm, stage, wext, rext):
    def make_perm(i, _):
        r = iota((64, PIX), 0) + i * 64
        c = iota((64, PIX), 1)
        hit = (c // CYC == r % ANG) & (c % CYC == r // ANG)
        perm[pl.ds(pl.multiple_of(i * 64, 64), 64), :] = onehot(hit)
        return 0

    lax.fori_loop(0, PIX // 64, make_perm, 0)

    def turn_rows(i, _):
        y = mm(part_ref[pl.ds(pl.multiple_of(i * 128, 128), 128), :], perm[...])
        for j in range(8):
            xs[pl.ds(i * 1024 + j, 128, stride=8), :] = y[:, j * 128 : (j + 1) * 128]
        return 0

    lax.fori_loop(0, TOK // 128, turn_rows, 0)
    for j in range(8):
        cs[pl.ds(j, KINDS, stride=8), :] = ctf_ref[:, j * 128 : (j + 1) * 128]
    square = ctf_ref[...] * ctf_ref[...]
    s1 = square.astype(BF16)
    s2 = (square - s1.astype(F32)).astype(BF16)
    for j in range(4):
        power[j * 32 : (j + 1) * 32, :] = s1 if j < 3 else jnp.zeros_like(s1)
        power[128 + j * 32 : 128 + (j + 1) * 32, :] = s2 if j < 3 else jnp.zeros_like(s2)
    ri = iota((128, 256), 0)
    ci = iota((128, 256), 1)
    want = (ci // 64) * CYC + ci % CYC
    rep = [onehot(ri == want + 64 * h) for h in range(2)]

    def spread_refs(g, _):
        flat = refs_ref[g]
        for h in range(2):
            spread[pl.ds(pl.multiple_of(g * 64 + h * 32, 32), 32), :] = mm(flat, rep[h]).astype(BF16)
        return 0

    lax.fori_loop(0, GROUPS, spread_refs, 0)
    out_ref[...] = jnp.zeros_like(out_ref)
    stage[...] = jnp.zeros_like(stage)
    lane = iota((1, 256), 1)
    masks = [onehot((lane // CYC) % 4 == b) for b in range(4)]
    half = iota((1, 128), 1) < 64
    lane_e = iota((1, 128), 1)
    k_row = iota((128, 128), 0)

    def group(g, _):
        base = spread[pl.ds(pl.multiple_of(g * 64, 64), 64), :]
        block = jnp.concatenate([base * m for m in masks], axis=0)
        for part in range(4):
            t = mm(rotq_ref[part * 256 : (part + 1) * 256, :], block)
            for pair in range(2):
                qp = part * 2 + pair
                for c in range(2):
                    a = t[pair * 128 : pair * 128 + 64, c * 128 : (c + 1) * 128]
                    b = t[pair * 128 + 64 : pair * 128 + 128, c * 128 : (c + 1) * 128]
                    e = jnp.where(half, a, pltpu.roll(b, 64, 1)).astype(BF16)
                    o = jnp.where(half, pltpu.roll(a, 64, 1), b).astype(BF16)
                    rext[c * 128 : c * 128 + 64, qp * 128 : (qp + 1) * 128] = e
                    rext[c * 128 + 64 : c * 128 + 128, qp * 128 : (qp + 1) * 128] = o
        rot = rext[:, 0:PIX]
        en = mm(rot * rot, power[...], NT)
        en = -0.5 * (en[:, 0:128] + en[:, 128:256])
        p1, p2, p3 = pieces(en)
        ext = jnp.where(lane_e < 32, p1.astype(F32), jnp.where(lane_e < 64, p2.astype(F32), jnp.where(lane_e < 96, p3.astype(F32), 0.0)))
        rext[:, PIX : PIX + 128] = ext.astype(BF16)
        def gather(i, _):
            for u in range(8):
                entry = tab_ref[g, i * 8 + u]
                p = entry % 1024
                k = entry // 1024
                x = xs[pl.ds(pl.multiple_of(p * 8, 8), 8), :]
                w = cs[pl.ds(pl.multiple_of(k * 8, 8), 8), :]
                stage[pl.ds(pl.multiple_of((i * 8 + u) * 8, 8), 8), :] = x * w
            return 0

        lax.fori_loop(0, tab_ref[g, SLOTS + 2] // 8, gather, 0)
        for j in range(8):
            col = stage[pl.ds(j, SLOTS, stride=8), :].astype(BF16)
            wext[:, j * 128 : (j + 1) * 128] = col
            wout_ref[g, :, j * 128 : (j + 1) * 128] = col
        kinds = kinds_ref[pl.ds(g, 1), :]
        hit = jnp.where(((k_row % 32) == kinds) & (k_row < 96), 1.0, 0.0)
        wext[:, PIX : PIX + 128] = jnp.transpose(hit)[0:SLOTS, :].astype(BF16)
        scores = mm(wext[...], rext[...], NT) * (4.0 / 64.0)
        out_ref[pl.ds(pl.multiple_of(tab_ref[g, SLOTS], 8), SLOTS), :] = scores
        return 0

    lax.fori_loop(0, GROUPS, group, 0)


def score_stage(tab, particles, refs, rotq, ctf, kinds):
    return pl.pallas_call(
        score_kernel,
        out_shape=(
            jax.ShapeDtypeStruct((PACKED, PAIRS), F32),
            jax.ShapeDtypeStruct((GROUPS, SLOTS, PIX), BF16),
        ),
        in_specs=[pl.BlockSpec(memory_space=pltpu.SMEM)] + vm(5),
        out_specs=tuple(vm(2)),
        scratch_shapes=[
            pltpu.VMEM((TOK * 8, 128), F32),
            pltpu.VMEM((KINDS * 8, 128), F32),
            pltpu.VMEM((GROUPS * 64, 256), BF16),
            pltpu.VMEM((256, PIX), BF16),
            pltpu.VMEM((PIX, PIX), BF16),
            pltpu.VMEM((SLOTS * 8, 128), F32),
            pltpu.VMEM((SLOTS, PIX + 128), BF16),
            pltpu.VMEM((PAIRS, PIX + 128), BF16),
        ],
        compiler_params=pltpu.CompilerParams(vmem_limit_bytes=VMEM_LIMIT),
        name="score_stage",
    )(tab, particles, refs, rotq, ctf, kinds)


def soft_kernel(part_ref, rho_ref, w_ref, log_ref, recv, stat, stat_recv, total, sems):
    me = lax.axis_index("cls")
    dom = lax.axis_index("dom")
    barrier = pltpu.get_barrier_semaphore()
    for d in range(1, SHARES):
        pl.semaphore_signal(barrier, inc=1, device_id=(lax.rem(me + d, SHARES), dom), device_id_type=MESH)
    pl.semaphore_wait(barrier, SHARES - 1)

    def copy(step, d, src, dst):
        return pltpu.make_async_remote_copy(
            src_ref=src,
            dst_ref=dst,
            send_sem=sems.at[step, 0, d],
            recv_sem=sems.at[step, 1, d],
            device_id=(lax.rem(me + d, SHARES), dom),
            device_id_type=MESH,
        )

    first = [copy(0, d, part_ref.at[lax.rem(me + d, SHARES)], recv.at[d - 1]) for d in (2, 1, 3)]
    for c in first:
        c.start()
    for c in first:
        c.wait()
    lanes = iota((64, 128), 1)
    top = jnp.zeros((64, 128), F32)
    tot = jnp.zeros((64, 128), F32)
    for j in range(HI):
        at = pl.ds(j * 64, 64)
        x = part_ref[me, at, :] + recv[0, at, :] + recv[1, at, :] + recv[2, at, :]
        total[at, :] = x
        m = jnp.max(x, axis=1, keepdims=True)
        s = jnp.sum(jnp.exp(x - m), axis=1, keepdims=True)
        here = lanes == me * HI + j
        top = jnp.where(here, m, top)
        tot = jnp.where(here, s, tot)
    stat[0] = top
    stat[1] = tot
    second = [copy(1, d, stat, stat_recv.at[d - 1]) for d in (2, 1, 3)]
    for c in second:
        c.start()
    for c in second:
        c.wait()
    top = stat[0] + stat_recv[0, 0] + stat_recv[1, 0] + stat_recv[2, 0]
    tot = stat[1] + stat_recv[0, 1] + stat_recv[1, 1] + stat_recv[2, 1]
    three = jnp.concatenate(list(pieces(top)) + list(pieces(tot)), axis=0)
    maxima, sums, his, los = [], [], [], []
    for j in range(2):
        rho = rho_ref[j : j + 1, :]
        hi = onehot(iota((128, TOK), 0) == rho // 64)
        lo = jnp.where(iota((64, TOK), 0) == rho % 64, 1.0, 0.0)
        t = mm(three, hi)
        maxima.append(jnp.sum((t[0:64] + t[64:128] + t[128:192]) * lo, axis=0, keepdims=True))
        sums.append(jnp.sum((t[192:256] + t[256:320] + t[320:384]) * lo, axis=0, keepdims=True))
        his.append(hi)
        los.append(lo)
    best = jnp.maximum(maxima[0], maxima[1])
    log = best + jnp.log(sums[0] * jnp.exp(maxima[0] - best) + sums[1] * jnp.exp(maxima[1] - best))
    log_ref[...] = log
    back = jnp.zeros((64, 128), F32)
    for j in range(2):
        for p in pieces(log):
            back = back + mm((los[j] * p.astype(F32)).astype(BF16), his[j], NT)
    for j in range(HI):
        at = pl.ds(j * 64, 64)
        col = jnp.sum(jnp.where(lanes == me * HI + j, back, 0.0), axis=1, keepdims=True)
        w_ref[me, at, :] = jnp.exp(total[at, :] - col).astype(BF16)
    third = [copy(2, d, w_ref.at[me], w_ref.at[me]) for d in (2, 1, 3)]
    for c in third:
        c.start()
    for c in third:
        c.wait()


def soft_stage(scores, rho):
    return pl.pallas_call(
        soft_kernel,
        out_shape=(
            jax.ShapeDtypeStruct((SHARES, ROWS, PAIRS), BF16),
            jax.ShapeDtypeStruct((1, TOK), F32),
        ),
        in_specs=vm(2),
        out_specs=tuple(vm(2)),
        scratch_shapes=[
            pltpu.VMEM((SHARES - 1, ROWS, PAIRS), F32),
            pltpu.VMEM((2, 64, 128), F32),
            pltpu.VMEM((SHARES - 1, 2, 64, 128), F32),
            pltpu.VMEM((ROWS, PAIRS), F32),
            pltpu.SemaphoreType.DMA((3, 2, SHARES)),
        ],
        compiler_params=pltpu.CompilerParams(collective_id=1, has_side_effects=True, vmem_limit_bytes=VMEM_LIMIT),
        name="soft_stage",
    )(scores.reshape(SHARES, ROWS, PAIRS), rho)


def turned_back(rows_of, rott_ref, rsq):
    half = iota((1, 128), 1) < 64
    for n in range(4):
        t = rows_of(n)
        for pair in range(2):
            qp = n * 2 + pair
            for c in range(2):
                a = t[c * 128 : c * 128 + 64, pair * 128 : (pair + 1) * 128]
                b = t[c * 128 + 64 : c * 128 + 128, pair * 128 : (pair + 1) * 128]
                e = jnp.where(half, a, pltpu.roll(b, 64, 1)).astype(BF16)
                o = jnp.where(half, pltpu.roll(a, 64, 1), b).astype(BF16)
                rsq[qp * 128 : qp * 128 + 64, c * 128 : (c + 1) * 128] = e
                rsq[qp * 128 + 64 : qp * 128 + 128, c * 128 : (c + 1) * 128] = o
    full = mm(rott_ref[...], rsq[...])
    lane = iota((1, 256), 1)
    diag = jnp.zeros((64, 256), F32)
    for b in range(4):
        diag = jnp.where((lane // CYC) % 4 == b, full[b * 64 : (b + 1) * 64, :], diag)
    ri = iota((256, 128), 0)
    ci = iota((256, 128), 1)
    want = (ri // 64) * CYC + ri % CYC
    p1 = diag.astype(BF16)
    p2 = (diag - p1.astype(F32)).astype(BF16)
    out = jnp.zeros((32, 128), F32)
    for h in range(2):
        fold = onehot(ci == want + 64 * h)
        out = out + mm(p1[h * 32 : (h + 1) * 32], fold) + mm(p2[h * 32 : (h + 1) * 32], fold)
    return out


def sum_kernel(tab_ref, w_ref, weighted_ref, rott_ref, kinds_ref, sums_ref, pk_ref, wide, rsq):
    me = lax.axis_index("cls")
    for i in range(SHARES):
        wide[i * ROWS : (i + 1) * ROWS, :] = w_ref[i].astype(F32)
    s_col = iota((SLOTS, PAIRS), 0)
    k_col = iota((8, 128), 0) + me * 8

    def group(g, _):
        at = pl.multiple_of(tab_ref[g, SLOTS], 8)
        w = wide[pl.ds(at, SLOTS), :]
        w = jnp.where(s_col < tab_ref[g, SLOTS + 1], w, 0.0)
        wt = jnp.transpose(w).astype(BF16)
        out = turned_back(lambda n: mm(wt, weighted_ref[g, :, n * 256 : (n + 1) * 256]), rott_ref, rsq)
        sums_ref[g] = out.astype(BF16)
        kinds = kinds_ref[pl.ds(g, 1), :]
        hit = onehot(k_col == kinds)[:, 0:SLOTS]
        pk_ref[g] = mm(hit, w.astype(BF16))
        return 0

    lax.fori_loop(0, GROUPS, group, 0)


def sum_stage(tab, w, weighted, rott, kinds):
    return pl.pallas_call(
        sum_kernel,
        out_shape=(
            jax.ShapeDtypeStruct((GROUPS, 32, 128), BF16),
            jax.ShapeDtypeStruct((GROUPS, 8, PAIRS), F32),
        ),
        in_specs=[pl.BlockSpec(memory_space=pltpu.SMEM)] + vm(4),
        out_specs=tuple(vm(2)),
        scratch_shapes=[
            pltpu.VMEM((PACKED, PAIRS), F32),
            pltpu.VMEM((1024, 256), BF16),
        ],
        compiler_params=pltpu.CompilerParams(vmem_limit_bytes=VMEM_LIMIT),
        name="sum_stage",
    )(tab, w, weighted, rott, kinds)


def end_kernel(sums_ref, pk_ref, ctf_ref, rott_ref, cs_ref, cw_ref, got, got_pk, mine, others, rsq, ssem, rsem, sems):
    me = lax.axis_index("dom")
    row = lax.axis_index("cls")
    barrier = pltpu.get_barrier_semaphore()

    def greet(i, _):
        pl.semaphore_signal(barrier, inc=1, device_id=(row, lax.rem(me + i, GROUPS)), device_id_type=MESH)
        return 0

    lax.fori_loop(1, GROUPS, greet, 0)
    for d in range(1, SHARES):
        pl.semaphore_signal(barrier, inc=1, device_id=(lax.rem(row + d, SHARES), me), device_id_type=MESH)
    pl.semaphore_wait(barrier, GROUPS - 1 + SHARES - 1)

    def copies(i):
        to = lax.rem(me + i, GROUPS)
        return [
            pltpu.make_async_remote_copy(
                src_ref=src.at[to],
                dst_ref=dst.at[i],
                send_sem=ssem.at[n, i],
                recv_sem=rsem.at[n, i],
                device_id=(row, to),
                device_id_type=MESH,
            )
            for n, (src, dst) in enumerate(((pk_ref, got_pk), (sums_ref, got)))
        ]

    def send(i, _):
        for c in copies(i):
            c.start()
        return 0

    lax.fori_loop(1, GROUPS, send, 0)

    def wait_pk(i, acc):
        copies(i)[0].wait()
        return acc + got_pk[i]

    acc = lax.fori_loop(1, GROUPS, wait_pk, pk_ref[me])
    mine[...] = acc

    def share(d):
        return pltpu.make_async_remote_copy(
            src_ref=mine,
            dst_ref=others.at[d - 1],
            send_sem=sems.at[0, d],
            recv_sem=sems.at[1, d],
            device_id=(lax.rem(row + d, SHARES), me),
            device_id_type=MESH,
        )

    for d in range(1, SHARES):
        share(d).start()

    def wait_sums(i, acc):
        copies(i)[1].wait()
        return acc + got[i].astype(F32)

    acc = lax.fori_loop(1, GROUPS, wait_sums, sums_ref[me].astype(F32))

    def placed(x, ref):
        t = jnp.transpose(x)
        ref[:, 0:32] = t[0:64, :].astype(ref.dtype)
        ref[:, 32:64] = t[64:128, :].astype(ref.dtype)

    placed(acc, cs_ref)
    for d in range(1, SHARES):
        share(d).wait()
    rows = []
    for k in range(SHARES):
        x = mine[...]
        for d in range(1, SHARES):
            x = jnp.where(lax.rem(k + d, SHARES) == row, others[d - 1], x)
        rows.append(x)
    pkt = jnp.transpose(jnp.concatenate(rows, axis=0))
    power = ctf_ref[...] * ctf_ref[...]

    def columns(n):
        return lax.dot_general(
            pkt, power[:, n * 256 : (n + 1) * 256], NN, precision=lax.Precision.HIGHEST, preferred_element_type=F32
        )

    placed(turned_back(columns, rott_ref, rsq), cw_ref)


def end_stage(sums, pk, ctf, rott):
    return pl.pallas_call(
        end_kernel,
        out_shape=(
            jax.ShapeDtypeStruct((64, 64), BF16),
            jax.ShapeDtypeStruct((64, 64), F32),
        ),
        in_specs=vm(4),
        out_specs=tuple(vm(2)),
        scratch_shapes=[
            pltpu.VMEM((GROUPS, 32, 128), BF16),
            pltpu.VMEM((GROUPS, 8, PAIRS), F32),
            pltpu.VMEM((8, PAIRS), F32),
            pltpu.VMEM((SHARES - 1, 8, PAIRS), F32),
            pltpu.VMEM((1024, 256), BF16),
            pltpu.SemaphoreType.DMA((2, GROUPS)),
            pltpu.SemaphoreType.DMA((2, GROUPS)),
            pltpu.SemaphoreType.DMA((2, SHARES)),
        ],
        compiler_params=pltpu.CompilerParams(collective_id=2, has_side_effects=True, vmem_limit_bytes=VMEM_LIMIT),
        name="end_stage",
    )(sums, pk, ctf, rott)


def prepared(candidates, defocus, ctf_table, references, rotations):
    mine = references.reshape(CPG, CYC, 2, 32).transpose(3, 2, 0, 1).reshape(32, 128)
    rotq = rotations.reshape(ROT, CYC, 4, ANG).transpose(1, 0, 2, 3).reshape(1024, 256)
    rott = rotq.T
    ctf = ctf_table.reshape(KINDS, CYC, ANG).transpose(0, 2, 1).reshape(KINDS, PIX)
    return mine, rotq, rott, ctf, candidates.T, defocus.reshape(1, TOK)


def local(particles, candidates, defocus, ctf_table, references, rotations):
    mine, rotq, rott, ctf, cand_t, kinds_row = prepared(candidates, defocus, ctf_table, references, rotations)
    tab, kinds, rho, refs = start_stage(cand_t, kinds_row, mine)
    scores, weighted = score_stage(tab, particles, refs, rotq, ctf, kinds)
    w, log = soft_stage(scores, rho)
    sums, pk = sum_stage(tab, w, weighted, rott, kinds)
    cs, cw = end_stage(sums, pk, ctf, rott)
    return cs.reshape(CPG, PIX), cw.reshape(CPG, PIX), log.reshape(TOK)


def solution(mesh):
    in_specs = (P("dom", "cls"), P("dom", None), P("dom"), P(None, "cls"), P("dom", "cls"), P())
    out_specs = (P("dom", "cls"), P("dom", "cls"), P("dom"))
    return jax.shard_map(local, mesh=mesh, in_specs=in_specs, out_specs=out_specs, check_vma=False)
```

time: 528 us -> 321 us (0.61)
  Pallas kernels: 0 us -> 308 us
  waiting for transfers between devices: 209 us -> 0 us
  local copies, waits for them, and re-layouts: 110 us -> 10.4 us
  matrix products: 63.2 us -> 0 us
  blocking collectives: 57.4 us -> 0 us
  starting transfers between devices: 49.8 us -> 0 us
  other arithmetic: 35.5 us -> 0 us
    pallas_call x0 -> x5, Pallas kernels: none -> 308 us  [the longest x1 114 us: score_stage(): pl.pallas_call(score_kernel, out_shape=(jax.ShapeDtypeStruct((PACKED, PAI...]
    all_to_all x5 -> x0, waiting for transfers between devices: 209 us -> none  [the longest x1 176 us: local(): lax.all_to_all(send_pixels, 'dom', split_axis=0, concat_axis=0, tiled=True)]
    gather x7 -> x0, local copies, waits for them, and re-layouts: 79 us -> none  [the longest x1 18.3 us: local(): particles[send_rows]]
    dot_general x24 -> x0, matrix products: 63.2 us -> none  [the longest x8 33 us: score_block(): ctf_rows = jnp.dot(picked_rows, ctf_table, precision=highest)]
    all_to_all x5 -> x0, starting transfers between devices: 49.8 us -> none  [the longest x1 17.8 us: sent_together(): lax.all_to_all(both, axis, split_axis=split_dim, concat_axis=concat_dim,...]
    all_to_all x1 -> x0, blocking collectives: 48.4 us -> none  [summed_on_arrival(): parts = lax.all_to_all(split_up(shard, dim, peers), axis, 0, 0, tiled=True)]
    another operation x3 -> x0, other arithmetic: 18.5 us -> none
    unnamed x20 -> x7, local copies, waits for them, and re-layouts: 9.83 us -> 0.61 us
  transfers between devices with their start and end apart: 5 -> 0, of which waited for: 4 -> 0; matrix products, arithmetic and copies ran while one was open for 8% -> 0% of each run, Pallas kernels for 0% -> 0%
where the time goes in v1:
time: 321 us; the launch traced here: 319 us
  Pallas kernels  308 us (96%)
  local copies, waits for them, and re-layouts  10.4 us (3%)
    pallas_call x1, Pallas kernels, score_stage(): pl.pallas_call(score_kernel, out_shape=(jax.ShapeDtypeStruct((PACKED, PAI...  114 us
    pallas_call x1, Pallas kernels, sum_stage(): pl.pallas_call(sum_kernel, out_shape=(jax.ShapeDtypeStruct((GROUPS, 32, 1...  67.8 us
    pallas_call x1, Pallas kernels, soft_stage(): pl.pallas_call(soft_kernel, out_shape=(jax.ShapeDtypeStruct((SHARES, ROWS...  59.2 us
    pallas_call x1, Pallas kernels, end_stage(): pl.pallas_call(end_kernel, out_shape=(jax.ShapeDtypeStruct((64, 64), BF16...  39.7 us
    pallas_call x1, Pallas kernels, start_stage(): pl.pallas_call(start_kernel, out_shape=(jax.ShapeDtypeStruct((GROUPS, 2 *...  27 us

profile of v1, /device:TPU:1, one launch (start us, length us, event | category | flops | bytes accessed | tf_op | source)
XLA Modules:
  0.0 318.9 jit_solution(1420109385265007434)
XLA Ops:
  0.6 0.0 copy-start.1
  0.6 0.9 reshape.40
  1.5 0.7 copy.14.mine_ref
  2.2 1.0 reshape.44
  3.2 0.3 copy.16
  3.5 0.8 copy.18.ctf_ref
  4.4 27.0 %start_stage.1 = (s32[64,128]{1,0:T(8,128)}, s32[64,128]{1,0:T(8,128)}, s32[2,1024]{1,0:T(2,128)}, bf16[64,32,128]{2,1,0:T(8,128)(2,1)}) custom-call(s32[2,1024]{1,0:T(2,128)} %bitcast.24, s32[1,1024]{1,0:T(1,128)} %bitcast.25, bf16[32,128]{1,0:T(8,128)(2,1)} %copy.14.mine_ref), custom_call_target="tpu_custom_call" | custom-call | tf_op jit(solution)/shard_map/start_stage/pallas_call | solution.py:140
  31.4 0.0 copy-done.1
  31.4 1.6 copy.15
  33.0 0.7 reshape.43
  33.7 0.0 copy-start
  33.7 1.0 copy.17.rotq_ref
  34.7 114.0 %score_stage.1 = (f32[2560,256]{1,0:T(8,128)}, bf16[64,64,1024]{2,1,0:T(8,128)(2,1)}) custom-call(s32[64,128]{1,0:T(8,128)} %get-tuple-element.15.tab_ref, bf16[1024,1024]{1,0:T(8,128)(2,1)} %part_ref.1, bf16[64,32,128]{2,1,0:T(8,128)(2,1)} %get-tuple-element.16.refs_ref, bf16[1024,256]{1,0:T(8,128)(2,1)} %copy.17.rotq_ref, f32[32,1024]{1,0:T(8,128)} %copy.18.ctf_ref, ...), custom_call_target="tpu_custom_call" | custom-call | tf_op jit(solution)/shard_map/score_stage/pallas_call | solution.py:251
  148.7 59.2 %soft_stage.1 = (bf16[4,640,256]{2,1,0:T(8,128)(2,1)}, f32[1,1024]{1,0:T(1,128)}) custom-call(f32[4,640,256]{2,1,0:T(8,128)} %bitcast.20, s32[2,1024]{1,0:T(2,128)} %get-tuple-element.19.rho_ref), custom_call_target="tpu_custom_call" | custom-call | tf_op jit(solution)/shard_map/soft_stage/pallas_call | solution.py:348
  207.9 0.0 copy-done
  207.9 0.0 copy-start.2
  207.9 67.8 %sum_stage.1 = (bf16[64,32,128]{2,1,0:T(8,128)(2,1)}, f32[64,8,256]{2,1,0:T(8,128)}) custom-call(s32[64,128]{1,0:T(8,128)} %get-tuple-element.15.tab_ref, bf16[4,640,256]{2,1,0:T(8,128)(2,1)} %get-tuple-element.20.w_ref, bf16[64,64,1024]{2,1,0:T(8,128)(2,1)} %get-tuple-element.21.weighted_ref, bf16[256,1024]{1,0:T(8,128)(2,1)} %bitcast.17, ...), custom_call_target="tpu_custom_call" | custom-call | tf_op jit(solution)/shard_map/sum_stage/pallas_call | solution.py:421
  275.7 39.7 %end_stage.1 = (bf16[64,64]{1,0:T(8,128)(2,1)}, f32[64,64]{1,0:T(8,128)}) custom-call(bf16[64,32,128]{2,1,0:T(8,128)(2,1)} %get-tuple-element.22.sums_ref, f32[64,8,256]{2,1,0:T(8,128)} %get-tuple-element.23.pk_ref, f32[32,1024]{1,0:T(8,128)} %copy.18.ctf_ref, bf16[256,1024]{1,0:T(8,128)(2,1)} %bitcast.18), custom_call_target="tpu_custom_call" | custom-call | tf_op jit(solution)/shard_map/end_stage/pallas_call | solution.py:525
  315.5 1.4 reshape.47
  316.9 1.4 reshape.48
  318.3 0.0 copy-done.2
  318.3 0.6 copy.21
  (1 shorter events, 0.0 us)
Async XLA Ops:
  0.6 30.8 %copy-start.1 = (bf16[64,64,64]{2,1,0:T(8,128)(2,1)S(1)}, bf16[64,64,64]{2,1,0:T(8,128)(2,1)}, u32[]{:S(2)}) copy-start(bf16[64,64,64]{2,1,0:T(8,128)(2,1)} %param.11) | copy-start | bytes 1572868
  33.7 174.2 %copy-start = (bf16[1024,256]{0,1:T(8,128)(2,1)}, bf16[1024,256]{0,1:T(8,128)(2,1)S(1)}, u32[]{:S(2)}) copy-start(bf16[1024,256]{0,1:T(8,128)(2,1)S(1)} %reshape.43) | copy-start | bytes 1572868
  207.9 110.4 %copy-start.2 = (f32[1,1024]{1,0:T(1,128)S(1)}, f32[1,1024]{1,0:T(1,128)}, u32[]{:S(2)}) copy-start(f32[1,1024]{1,0:T(1,128)} %get-tuple-element.26) | copy-start | bytes 12292

commit v2 on v1

--- a/solution.py
+++ b/solution.py
@@ -90,14 +90,33 @@
     token = high.astype(I32) * 8 + low_int // 32
     s_lane = iota((GROUPS, SLOTS), 1)
     live = s_lane < count.astype(I32)
-    tab_ref[:, 0:SLOTS] = token + 1024 * kinds
+    tab_ref[:, 0:SLOTS] = token * 8 + 65536 * 8 * kinds
     extra = jnp.where(s_lane == 0, offset, jnp.where(s_lane == 1, count, padded))
     tab_ref[:, SLOTS : 2 * SLOTS] = extra.astype(I32)
     kinds_ref[:, 0:SLOTS] = jnp.where(live, kinds, -1)
     kinds_ref[:, SLOTS : 2 * SLOTS] = jnp.full((GROUPS, SLOTS), -1, I32)
 
 
-def start_kernel(cand_ref, kind_ref, mine_ref, tab_ref, kinds_ref, rho_ref, all_ref, send_sem, recv_sem, own_sem):
+def turn_pixels(part_ref, xs_ref, perm):
+    def make_perm(i, _):
+        r = iota((64, PIX), 0)
+        c = iota((64, PIX), 1)
+        hit = c == (r * CYC + i)
+        perm[pl.ds(pl.multiple_of(i * 64, 64), 64), :] = onehot(hit)
+        return 0
+
+    lax.fori_loop(0, CYC, make_perm, 0)
+
+    def turn_rows(i, _):
+        y = mm(part_ref[pl.ds(pl.multiple_of(i * 128, 128), 128), :], perm[...])
+        for j in range(8):
+            xs_ref[pl.ds(i * 1024 + j, 128, stride=8), :] = y[:, j * 128 : (j + 1) * 128]
+        return 0
+
+    lax.fori_loop(0, TOK // 128, turn_rows, 0)
+
+
+def start_kernel(cand_ref, kind_ref, mine_ref, part_ref, tab_ref, kinds_ref, rho_ref, all_ref, xs_ref, perm, send_sem, recv_sem, own_sem):
     me = lax.axis_index("dom")
     row = lax.axis_index("cls")
     barrier = pltpu.get_barrier_semaphore()
@@ -127,6 +146,7 @@
     own = pltpu.make_async_copy(mine_ref, all_ref.at[me], own_sem)
     own.start()
     route(cand_ref, kind_ref, tab_ref, kinds_ref, rho_ref)
+    turn_pixels(part_ref, xs_ref, perm)
     own.wait()
 
     def finish(i, _):
@@ -136,7 +156,7 @@
     lax.fori_loop(1, GROUPS, finish, 0)
 
 
-def start_stage(cand_t, kinds_row, mine):
+def start_stage(cand_t, kinds_row, mine, particles):
     return pl.pallas_call(
         start_kernel,
         out_shape=(
@@ -144,110 +164,108 @@
             jax.ShapeDtypeStruct((GROUPS, 2 * SLOTS), I32),
             jax.ShapeDtypeStruct((2, TOK), I32),
             jax.ShapeDtypeStruct((GROUPS, 32, 128), BF16),
+            jax.ShapeDtypeStruct((TOK * 8, 128), F32),
         ),
-        in_specs=vm(3),
-        out_specs=tuple(vm(4)),
+        in_specs=vm(4),
+        out_specs=tuple(vm(5)),
         scratch_shapes=[
+            pltpu.VMEM((PIX, PIX), BF16),
             pltpu.SemaphoreType.DMA((GROUPS,)),
             pltpu.SemaphoreType.DMA((GROUPS,)),
             pltpu.SemaphoreType.DMA,
         ],
         compiler_params=pltpu.CompilerParams(collective_id=0, has_side_effects=True, vmem_limit_bytes=VMEM_LIMIT),
         name="start_stage",
-    )(cand_t, kinds_row, mine)
-
-
-def score_kernel(tab_ref, part_ref, refs_ref, rotq_ref, ctf_ref, kinds_ref, out_ref, wout_ref, xs, cs, spread, power, perm, stage, wext, rext):
-    def make_perm(i, _):
-        r = iota((64, PIX), 0) + i * 64
-        c = iota((64, PIX), 1)
-        hit = (c // CYC == r % ANG) & (c % CYC == r // ANG)
-        perm[pl.ds(pl.multiple_of(i * 64, 64), 64), :] = onehot(hit)
-        return 0
-
-    lax.fori_loop(0, PIX // 64, make_perm, 0)
-
-    def turn_rows(i, _):
-        y = mm(part_ref[pl.ds(pl.multiple_of(i * 128, 128), 128), :], perm[...])
-        for j in range(8):
-            xs[pl.ds(i * 1024 + j, 128, stride=8), :] = y[:, j * 128 : (j + 1) * 128]
-        return 0
-
-    lax.fori_loop(0, TOK // 128, turn_rows, 0)
+    )(cand_t, kinds_row, mine, particles)
+
+
+def score_kernel(tab_ref, xs, refs_ref, rott_ref, ctf_ref, kinds_ref, out_ref, wout_ref, cs, power, bd, raw, rot_a, rot_b, stage_a, stage_b, weights_a, weights_b, hits_a, hits_b):
+    rots, stages, weights, hits = (rot_a, rot_b), (stage_a, stage_b), (weights_a, weights_b), (hits_a, hits_b)
     for j in range(8):
         cs[pl.ds(j, KINDS, stride=8), :] = ctf_ref[:, j * 128 : (j + 1) * 128]
-    square = ctf_ref[...] * ctf_ref[...]
+    square = -0.5 * (ctf_ref[...] * ctf_ref[...])
     s1 = square.astype(BF16)
-    s2 = (square - s1.astype(F32)).astype(BF16)
-    for j in range(4):
-        power[j * 32 : (j + 1) * 32, :] = s1 if j < 3 else jnp.zeros_like(s1)
-        power[128 + j * 32 : 128 + (j + 1) * 32, :] = s2 if j < 3 else jnp.zeros_like(s2)
-    ri = iota((128, 256), 0)
-    ci = iota((128, 256), 1)
-    want = (ci // 64) * CYC + ci % CYC
-    rep = [onehot(ri == want + 64 * h) for h in range(2)]
-
-    def spread_refs(g, _):
-        flat = refs_ref[g]
-        for h in range(2):
-            spread[pl.ds(pl.multiple_of(g * 64 + h * 32, 32), 32), :] = mm(flat, rep[h]).astype(BF16)
-        return 0
-
-    lax.fori_loop(0, GROUPS, spread_refs, 0)
+    power[0:32, :] = s1
+    power[32:64, :] = (square - s1.astype(F32)).astype(BF16)
     out_ref[...] = jnp.zeros_like(out_ref)
-    stage[...] = jnp.zeros_like(stage)
-    lane = iota((1, 256), 1)
-    masks = [onehot((lane // CYC) % 4 == b) for b in range(4)]
+    bd[...] = jnp.zeros_like(bd)
     half = iota((1, 128), 1) < 64
-    lane_e = iota((1, 128), 1)
+    keep = jnp.broadcast_to(half, (64, 128))
+    keep_16 = jnp.broadcast_to(half, (16, 128))
+    blank = jnp.zeros((16, 128), BF16)
     k_row = iota((128, 128), 0)
 
-    def group(g, _):
-        base = spread[pl.ds(pl.multiple_of(g * 64, 64), 64), :]
-        block = jnp.concatenate([base * m for m in masks], axis=0)
-        for part in range(4):
-            t = mm(rotq_ref[part * 256 : (part + 1) * 256, :], block)
-            for pair in range(2):
-                qp = part * 2 + pair
-                for c in range(2):
-                    a = t[pair * 128 : pair * 128 + 64, c * 128 : (c + 1) * 128]
-                    b = t[pair * 128 + 64 : pair * 128 + 128, c * 128 : (c + 1) * 128]
-                    e = jnp.where(half, a, pltpu.roll(b, 64, 1)).astype(BF16)
-                    o = jnp.where(half, pltpu.roll(a, 64, 1), b).astype(BF16)
-                    rext[c * 128 : c * 128 + 64, qp * 128 : (qp + 1) * 128] = e
-                    rext[c * 128 + 64 : c * 128 + 128, qp * 128 : (qp + 1) * 128] = o
-        rot = rext[:, 0:PIX]
-        en = mm(rot * rot, power[...], NT)
-        en = -0.5 * (en[:, 0:128] + en[:, 128:256])
-        p1, p2, p3 = pieces(en)
-        ext = jnp.where(lane_e < 32, p1.astype(F32), jnp.where(lane_e < 64, p2.astype(F32), jnp.where(lane_e < 96, p3.astype(F32), 0.0)))
-        rext[:, PIX : PIX + 128] = ext.astype(BF16)
-        def gather(i, _):
-            for u in range(8):
-                entry = tab_ref[g, i * 8 + u]
-                p = entry % 1024
-                k = entry // 1024
-                x = xs[pl.ds(pl.multiple_of(p * 8, 8), 8), :]
-                w = cs[pl.ds(pl.multiple_of(k * 8, 8), 8), :]
-                stage[pl.ds(pl.multiple_of((i * 8 + u) * 8, 8), 8), :] = x * w
-            return 0
-
-        lax.fori_loop(0, tab_ref[g, SLOTS + 2] // 8, gather, 0)
+    def rotate(pair):
+        for u in range(2):
+            for cl in range(2):
+                x = refs_ref[pair * 2 + u, cl * 16 : (cl + 1) * 16, :]
+                y = pltpu.roll(x, 64, 1)
+                for ch, (low, high) in enumerate(((x, y), (y, x))):
+                    at = u * 256 + (ch * 2 + cl) * 64
+                    low = jnp.where(keep_16, low, blank)
+                    high = jnp.where(keep_16, blank, high)
+                    bd[at : at + 16, 0:128] = low
+                    bd[at + 16 : at + 32, 0:128] = high
+                    bd[at + 32 : at + 48, 128:256] = low
+                    bd[at + 48 : at + 64, 128:256] = high
+        for n in range(4):
+            at = slice(n * 256, (n + 1) * 256)
+            raw[:, at] = mm(bd[...], rott_ref[:, at]).astype(BF16)
+
+    def arrange(pair, u):
+        g = pair * 2 + u
+        rot, stage, weighted = rots[u], stages[u], weights[u]
+        for s in range(SLOTS):
+            entry = tab_ref[g, s]
+            p = entry & 65535
+            k = lax.shift_right_logical(entry, 16)
+            x = xs[pl.ds(pl.multiple_of(p, 8), 8), :]
+            w = cs[pl.ds(pl.multiple_of(k, 8), 8), :]
+            stage[s * 8 : (s + 1) * 8, :] = x * w
+        for qp in range(8):
+            for k in range(2):
+                r0 = u * 256 + k * 128
+                a = raw[r0 : r0 + 64, qp * 128 : (qp + 1) * 128]
+                b = raw[r0 + 64 : r0 + 128, qp * 128 : (qp + 1) * 128]
+                rot[qp * 128 : qp * 128 + 64, k * 128 : (k + 1) * 128] = jnp.where(keep, a, pltpu.roll(b, 64, 1))
+                rot[qp * 128 + 64 : qp * 128 + 128, k * 128 : (k + 1) * 128] = jnp.where(keep, pltpu.roll(a, 64, 1), b)
         for j in range(8):
             col = stage[pl.ds(j, SLOTS, stride=8), :].astype(BF16)
-            wext[:, j * 128 : (j + 1) * 128] = col
+            weighted[:, j * 128 : (j + 1) * 128] = col
             wout_ref[g, :, j * 128 : (j + 1) * 128] = col
         kinds = kinds_ref[pl.ds(g, 1), :]
-        hit = jnp.where(((k_row % 32) == kinds) & (k_row < 96), 1.0, 0.0)
-        wext[:, PIX : PIX + 128] = jnp.transpose(hit)[0:SLOTS, :].astype(BF16)
-        scores = mm(wext[...], rext[...], NT) * (4.0 / 64.0)
-        out_ref[pl.ds(pl.multiple_of(tab_ref[g, SLOTS], 8), SLOTS), :] = scores
-        return 0
-
-    lax.fori_loop(0, GROUPS, group, 0)
-
-
-def score_stage(tab, particles, refs, rotq, ctf, kinds):
+        hit = jnp.where(((k_row & 31) == kinds) & (k_row < 64), 1.0, 0.0)
+        hits[u][...] = jnp.transpose(hit)[0:SLOTS, :].astype(BF16)
+
+    def score(pair, u):
+        g = pair * 2 + u
+        rot, weighted = rots[u], weights[u]
+        en, total = None, None
+        for part in range(2):
+            at = slice(part * 512, (part + 1) * 512)
+            r = rot[at, :]
+            z = mm(weighted[:, at], r)
+            y = mm(power[:, at], r * r)
+            total = z if total is None else total + z
+            en = y if en is None else en + y
+        en = en[0:32, :] + en[32:64, :]
+        p1 = en.astype(BF16)
+        p2 = (en - p1.astype(F32)).astype(BF16)
+        total = total + mm(hits[u][:, 0:64], jnp.concatenate([p1, p2], axis=0))
+        out_ref[pl.ds(pl.multiple_of(tab_ref[g, SLOTS], 8), SLOTS), :] = total * (4.0 / 64.0)
+
+    def step(t, _):
+        for u in range(2):
+            score(jnp.clip(t - 2, 0, GROUPS // 2 - 1), u)
+        for u in range(2):
+            arrange(jnp.clip(t - 1, 0, GROUPS // 2 - 1), u)
+        rotate(jnp.minimum(t, GROUPS // 2 - 1))
+        return 0
+
+    lax.fori_loop(0, GROUPS // 2 + 2, step, 0)
+
+
+def score_stage(tab, xs, refs, rott, ctf, kinds):
     return pl.pallas_call(
         score_kernel,
         out_shape=(
@@ -257,21 +275,25 @@
         in_specs=[pl.BlockSpec(memory_space=pltpu.SMEM)] + vm(5),
         out_specs=tuple(vm(2)),
         scratch_shapes=[
-            pltpu.VMEM((TOK * 8, 128), F32),
             pltpu.VMEM((KINDS * 8, 128), F32),
-            pltpu.VMEM((GROUPS * 64, 256), BF16),
-            pltpu.VMEM((256, PIX), BF16),
-            pltpu.VMEM((PIX, PIX), BF16),
+            pltpu.VMEM((64, PIX), BF16),
+            pltpu.VMEM((512, 256), BF16),
+            pltpu.VMEM((512, PIX), BF16),
+            pltpu.VMEM((PIX, PAIRS), BF16),
+            pltpu.VMEM((PIX, PAIRS), BF16),
             pltpu.VMEM((SLOTS * 8, 128), F32),
-            pltpu.VMEM((SLOTS, PIX + 128), BF16),
-            pltpu.VMEM((PAIRS, PIX + 128), BF16),
+            pltpu.VMEM((SLOTS * 8, 128), F32),
+            pltpu.VMEM((SLOTS, PIX), BF16),
+            pltpu.VMEM((SLOTS, PIX), BF16),
+            pltpu.VMEM((SLOTS, 128), BF16),
+            pltpu.VMEM((SLOTS, 128), BF16),
         ],
         compiler_params=pltpu.CompilerParams(vmem_limit_bytes=VMEM_LIMIT),
         name="score_stage",
-    )(tab, particles, refs, rotq, ctf, kinds)
-
-
-def soft_kernel(part_ref, rho_ref, w_ref, log_ref, recv, stat, stat_recv, total, sems):
+    )(tab, xs, refs, rott, ctf, kinds)
+
+
+def soft_kernel(part_ref, rho_ref, w_ref, log_ref, far, held, near, stat, stat_recv, total, sems, ring):
     me = lax.axis_index("cls")
     dom = lax.axis_index("dom")
     barrier = pltpu.get_barrier_semaphore()
@@ -289,17 +311,41 @@
             device_id_type=MESH,
         )
 
-    first = [copy(0, d, part_ref.at[lax.rem(me + d, SHARES)], recv.at[d - 1]) for d in (2, 1, 3)]
-    for c in first:
+    right, left, across = lax.rem(me + 1, SHARES), lax.rem(me + 3, SHARES), lax.rem(me + 2, SHARES)
+    low, high = pl.ds(0, ROWS // 2), pl.ds(ROWS // 2, ROWS // 2)
+
+    def hop(n, to, src, dst):
+        return pltpu.make_async_remote_copy(
+            src_ref=src,
+            dst_ref=dst,
+            send_sem=ring.at[0, n],
+            recv_sem=ring.at[1, n],
+            device_id=(to, dom),
+            device_id_type=MESH,
+        )
+
+    out_low = hop(0, right, part_ref.at[across, low], far.at[0])
+    out_high = hop(1, left, part_ref.at[across, high], far.at[1])
+    to_right = hop(2, right, part_ref.at[right, high], near.at[0, high])
+    to_left = hop(3, left, part_ref.at[left, low], near.at[1, low])
+    for c in (out_low, out_high, to_right, to_left):
         c.start()
-    for c in first:
+    out_low.wait()
+    held[0] = part_ref[right, low, :] + far[0]
+    sum_right = hop(4, right, held.at[0], near.at[0, low])
+    sum_right.start()
+    out_high.wait()
+    held[1] = part_ref[left, high, :] + far[1]
+    sum_left = hop(5, left, held.at[1], near.at[1, high])
+    sum_left.start()
+    for c in (to_right, to_left, sum_right, sum_left):
         c.wait()
     lanes = iota((64, 128), 1)
     top = jnp.zeros((64, 128), F32)
     tot = jnp.zeros((64, 128), F32)
     for j in range(HI):
         at = pl.ds(j * 64, 64)
-        x = part_ref[me, at, :] + recv[0, at, :] + recv[1, at, :] + recv[2, at, :]
+        x = part_ref[me, at, :] + near[0, at, :] + near[1, at, :]
         total[at, :] = x
         m = jnp.max(x, axis=1, keepdims=True)
         s = jnp.sum(jnp.exp(x - m), axis=1, keepdims=True)
@@ -337,11 +383,18 @@
         at = pl.ds(j * 64, 64)
         col = jnp.sum(jnp.where(lanes == me * HI + j, back, 0.0), axis=1, keepdims=True)
         w_ref[me, at, :] = jnp.exp(total[at, :] - col).astype(BF16)
-    third = [copy(2, d, w_ref.at[me], w_ref.at[me]) for d in (2, 1, 3)]
-    for c in third:
-        c.start()
-    for c in third:
-        c.wait()
+    own_right = hop(6, right, w_ref.at[me], w_ref.at[me])
+    own_left = hop(7, left, w_ref.at[me], w_ref.at[me])
+    own_right.start()
+    own_left.start()
+    own_right.wait()
+    on_right = hop(8, right, w_ref.at[left, low], w_ref.at[left, low])
+    on_right.start()
+    own_left.wait()
+    on_left = hop(9, left, w_ref.at[right, high], w_ref.at[right, high])
+    on_left.start()
+    on_right.wait()
+    on_left.wait()
 
 
 def soft_stage(scores, rho):
@@ -354,67 +407,109 @@
         in_specs=vm(2),
         out_specs=tuple(vm(2)),
         scratch_shapes=[
-            pltpu.VMEM((SHARES - 1, ROWS, PAIRS), F32),
+            pltpu.VMEM((2, ROWS // 2, PAIRS), F32),
+            pltpu.VMEM((2, ROWS // 2, PAIRS), F32),
+            pltpu.VMEM((2, ROWS, PAIRS), F32),
             pltpu.VMEM((2, 64, 128), F32),
             pltpu.VMEM((SHARES - 1, 2, 64, 128), F32),
             pltpu.VMEM((ROWS, PAIRS), F32),
-            pltpu.SemaphoreType.DMA((3, 2, SHARES)),
+            pltpu.SemaphoreType.DMA((2, 2, SHARES)),
+            pltpu.SemaphoreType.DMA((2, 10)),
         ],
         compiler_params=pltpu.CompilerParams(collective_id=1, has_side_effects=True, vmem_limit_bytes=VMEM_LIMIT),
         name="soft_stage",
     )(scores.reshape(SHARES, ROWS, PAIRS), rho)
 
 
-def turned_back(rows_of, rott_ref, rsq):
-    half = iota((1, 128), 1) < 64
-    for n in range(4):
-        t = rows_of(n)
-        for pair in range(2):
-            qp = n * 2 + pair
-            for c in range(2):
-                a = t[c * 128 : c * 128 + 64, pair * 128 : (pair + 1) * 128]
-                b = t[c * 128 + 64 : c * 128 + 128, pair * 128 : (pair + 1) * 128]
-                e = jnp.where(half, a, pltpu.roll(b, 64, 1)).astype(BF16)
-                o = jnp.where(half, pltpu.roll(a, 64, 1), b).astype(BF16)
-                rsq[qp * 128 : qp * 128 + 64, c * 128 : (c + 1) * 128] = e
-                rsq[qp * 128 + 64 : qp * 128 + 128, c * 128 : (c + 1) * 128] = o
-    full = mm(rott_ref[...], rsq[...])
+def turned(raw, rsq):
+    keep = jnp.broadcast_to(iota((1, 128), 1) < 64, (64, 128))
+    for qp in range(8):
+        for c in range(2):
+            a = raw[c * 128 : c * 128 + 64, qp * 128 : (qp + 1) * 128]
+            b = raw[c * 128 + 64 : c * 128 + 128, qp * 128 : (qp + 1) * 128]
+            e = jnp.where(keep, a, pltpu.roll(b, 64, 1))
+            o = jnp.where(keep, pltpu.roll(a, 64, 1), b)
+            rsq[qp * 128 : qp * 128 + 64, c * 128 : (c + 1) * 128] = e
+            rsq[qp * 128 + 64 : qp * 128 + 128, c * 128 : (c + 1) * 128] = o
+
+
+def diagonal(rott_ref, rsq):
     lane = iota((1, 256), 1)
-    diag = jnp.zeros((64, 256), F32)
-    for b in range(4):
-        diag = jnp.where((lane // CYC) % 4 == b, full[b * 64 : (b + 1) * 64, :], diag)
+    total = None
+    for part in range(2):
+        at = slice(part * 512, (part + 1) * 512)
+        full = mm(rott_ref[:, at], rsq[at, :])
+        diag = full[0:64, :]
+        for b in range(1, 4):
+            diag = jnp.where((lane // CYC) % 4 == b, full[b * 64 : (b + 1) * 64, :], diag)
+        total = diag if total is None else total + diag
+    return total
+
+
+def folds():
     ri = iota((256, 128), 0)
     ci = iota((256, 128), 1)
     want = (ri // 64) * CYC + ri % CYC
-    p1 = diag.astype(BF16)
-    p2 = (diag - p1.astype(F32)).astype(BF16)
-    out = jnp.zeros((32, 128), F32)
-    for h in range(2):
-        fold = onehot(ci == want + 64 * h)
-        out = out + mm(p1[h * 32 : (h + 1) * 32], fold) + mm(p2[h * 32 : (h + 1) * 32], fold)
+    return [onehot(ci == want + 64 * h) for h in range(2)]
+
+
+def folded(parts, fold):
+    out = None
+    for x, f in zip(parts, fold):
+        p1 = x.astype(BF16)
+        p2 = (x - p1.astype(F32)).astype(BF16)
+        y = mm(p1, f) + mm(p2, f)
+        out = y if out is None else out + y
     return out
 
 
-def sum_kernel(tab_ref, w_ref, weighted_ref, rott_ref, kinds_ref, sums_ref, pk_ref, wide, rsq):
+def sum_kernel(tab_ref, w_ref, weighted_ref, rott_ref, kinds_ref, sums_ref, pk_ref, wide, rsq_a, rsq_b, raw_a, raw_b, parts):
+    rsqs, raws = (rsq_a, rsq_b), (raw_a, raw_b)
     me = lax.axis_index("cls")
     for i in range(SHARES):
         wide[i * ROWS : (i + 1) * ROWS, :] = w_ref[i].astype(F32)
     s_col = iota((SLOTS, PAIRS), 0)
     k_col = iota((8, 128), 0) + me * 8
 
-    def group(g, _):
+    def spread_out(g, raw):
         at = pl.multiple_of(tab_ref[g, SLOTS], 8)
         w = wide[pl.ds(at, SLOTS), :]
         w = jnp.where(s_col < tab_ref[g, SLOTS + 1], w, 0.0)
         wt = jnp.transpose(w).astype(BF16)
-        out = turned_back(lambda n: mm(wt, weighted_ref[g, :, n * 256 : (n + 1) * 256]), rott_ref, rsq)
-        sums_ref[g] = out.astype(BF16)
+        for n in range(4):
+            at = slice(n * 256, (n + 1) * 256)
+            raw[:, at] = mm(wt, weighted_ref[g, :, at]).astype(BF16)
         kinds = kinds_ref[pl.ds(g, 1), :]
         hit = onehot(k_col == kinds)[:, 0:SLOTS]
         pk_ref[g] = mm(hit, w.astype(BF16))
-        return 0
-
-    lax.fori_loop(0, GROUPS, group, 0)
+
+    def finish(g, rsq):
+        diag = diagonal(rott_ref, rsq)
+        for h in range(2):
+            parts[h, pl.ds(pl.multiple_of(g * 32, 32), 32), :] = diag[h * 32 : (h + 1) * 32, :]
+
+    def two(i, _):
+        for odd in range(2):
+            t = i * 2 + odd
+            now, other = odd, 1 - odd
+            last = jnp.clip(t - 2, 0, GROUPS - 1)
+            new = jnp.minimum(t, GROUPS - 1)
+            finish(last, rsqs[now])
+            turned(raws[other], rsqs[other])
+            spread_out(new, raws[now])
+        return 0
+
+    lax.fori_loop(0, GROUPS // 2 + 1, two, 0)
+    fold = folds()
+
+    def fold_eight(i, _):
+        at = pl.ds(pl.multiple_of(i * 256, 256), 256)
+        out = folded([parts[h, at, :] for h in range(2)], fold).astype(BF16)
+        for j in range(8):
+            sums_ref[i * 8 + j] = out[j * 32 : (j + 1) * 32, :]
+        return 0
+
+    lax.fori_loop(0, GROUPS // 8, fold_eight, 0)
 
 
 def sum_stage(tab, w, weighted, rott, kinds):
@@ -429,13 +524,17 @@
         scratch_shapes=[
             pltpu.VMEM((PACKED, PAIRS), F32),
             pltpu.VMEM((1024, 256), BF16),
+            pltpu.VMEM((1024, 256), BF16),
+            pltpu.VMEM((PAIRS, PIX), BF16),
+            pltpu.VMEM((PAIRS, PIX), BF16),
+            pltpu.VMEM((2, GROUPS * 32, 256), F32),
         ],
         compiler_params=pltpu.CompilerParams(vmem_limit_bytes=VMEM_LIMIT),
         name="sum_stage",
     )(tab, w, weighted, rott, kinds)
 
 
-def end_kernel(sums_ref, pk_ref, ctf_ref, rott_ref, cs_ref, cw_ref, got, got_pk, mine, others, rsq, ssem, rsem, sems):
+def end_kernel(sums_ref, pk_ref, ctf_ref, rott_ref, cs_ref, cw_ref, got, got_pk, mine, others, rsq, raw, ssem, rsem, sems):
     me = lax.axis_index("dom")
     row = lax.axis_index("cls")
     barrier = pltpu.get_barrier_semaphore()
@@ -513,12 +612,14 @@
     pkt = jnp.transpose(jnp.concatenate(rows, axis=0))
     power = ctf_ref[...] * ctf_ref[...]
 
-    def columns(n):
-        return lax.dot_general(
-            pkt, power[:, n * 256 : (n + 1) * 256], NN, precision=lax.Precision.HIGHEST, preferred_element_type=F32
-        )
-
-    placed(turned_back(columns, rott_ref, rsq), cw_ref)
+    for n in range(4):
+        at = slice(n * 256, (n + 1) * 256)
+        raw[:, at] = lax.dot_general(
+            pkt, power[:, at], NN, precision=lax.Precision.HIGHEST, preferred_element_type=F32
+        ).astype(BF16)
+    turned(raw, rsq)
+    diag = diagonal(rott_ref, rsq)
+    placed(folded([diag[0:32], diag[32:64]], folds()), cw_ref)
 
 
 def end_stage(sums, pk, ctf, rott):
@@ -536,6 +637,7 @@
             pltpu.VMEM((8, PAIRS), F32),
             pltpu.VMEM((SHARES - 1, 8, PAIRS), F32),
             pltpu.VMEM((1024, 256), BF16),
+            pltpu.VMEM((PAIRS, PIX), BF16),
             pltpu.SemaphoreType.DMA((2, GROUPS)),
             pltpu.SemaphoreType.DMA((2, GROUPS)),
             pltpu.SemaphoreType.DMA((2, SHARES)),
@@ -546,17 +648,16 @@
 
 
 def prepared(candidates, defocus, ctf_table, references, rotations):
-    mine = references.reshape(CPG, CYC, 2, 32).transpose(3, 2, 0, 1).reshape(32, 128)
-    rotq = rotations.reshape(ROT, CYC, 4, ANG).transpose(1, 0, 2, 3).reshape(1024, 256)
-    rott = rotq.T
+    mine = references.reshape(2, 2, CYC, ANG).transpose(1, 2, 0, 3).reshape(32, 128)
+    rott = rotations.reshape(ROT, CYC, 4 * ANG).transpose(2, 1, 0).reshape(256, 1024)
     ctf = ctf_table.reshape(KINDS, CYC, ANG).transpose(0, 2, 1).reshape(KINDS, PIX)
-    return mine, rotq, rott, ctf, candidates.T, defocus.reshape(1, TOK)
+    return mine, rott, ctf, candidates.T, defocus.reshape(1, TOK)
 
 
 def local(particles, candidates, defocus, ctf_table, references, rotations):
-    mine, rotq, rott, ctf, cand_t, kinds_row = prepared(candidates, defocus, ctf_table, references, rotations)
-    tab, kinds, rho, refs = start_stage(cand_t, kinds_row, mine)
-    scores, weighted = score_stage(tab, particles, refs, rotq, ctf, kinds)
+    mine, rott, ctf, cand_t, kinds_row = prepared(candidates, defocus, ctf_table, references, rotations)
+    tab, kinds, rho, refs, xs = start_stage(cand_t, kinds_row, mine, particles)
+    scores, weighted = score_stage(tab, xs, refs, rott, ctf, kinds)
     w, log = soft_stage(scores, rho)
     sums, pk = sum_stage(tab, w, weighted, rott, kinds)
     cs, cw = end_stage(sums, pk, ctf, rott)

time: 321 us -> 208 us (0.65)
  Pallas kernels: 308 us -> 197 us
    pallas_call x1, Pallas kernels: 114 us -> 43.8 us  [score_stage(): pl.pallas_call(score_kernel, out_shape=(jax.ShapeDtypeStruct((PACKED, PAI...]
    pallas_call x1, Pallas kernels: 67.8 us -> 33.7 us  [sum_stage(): pl.pallas_call(sum_kernel, out_shape=(jax.ShapeDtypeStruct((GROUPS, 32, 1...]
    pallas_call x1, Pallas kernels: 59.2 us -> 45.6 us  [soft_stage(): pl.pallas_call(soft_kernel, out_shape=(jax.ShapeDtypeStruct((SHARES, ROWS...]
    pallas_call x1, Pallas kernels: 39.7 us -> 45 us  [end_stage(): pl.pallas_call(end_kernel, out_shape=(jax.ShapeDtypeStruct((64, 64), BF16...]
where the time goes in v2:
time: 208 us; the launch traced here: 207 us
  Pallas kernels  197 us (95%)
  local copies, waits for them, and re-layouts  9.01 us (4%)
    pallas_call x1, Pallas kernels, soft_stage(): pl.pallas_call(soft_kernel, out_shape=(jax.ShapeDtypeStruct((SHARES, ROWS...  45.6 us
    pallas_call x1, Pallas kernels, end_stage(): pl.pallas_call(end_kernel, out_shape=(jax.ShapeDtypeStruct((64, 64), BF16...  45 us
    pallas_call x1, Pallas kernels, score_stage(): pl.pallas_call(score_kernel, out_shape=(jax.ShapeDtypeStruct((PACKED, PAI...  43.8 us
    pallas_call x1, Pallas kernels, sum_stage(): pl.pallas_call(sum_kernel, out_shape=(jax.ShapeDtypeStruct((GROUPS, 32, 1...  33.7 us
    pallas_call x1, Pallas kernels, start_stage(): pl.pallas_call(start_kernel, out_shape=(jax.ShapeDtypeStruct((GROUPS, 2 *...  29.2 us

profile of v2, /device:TPU:1, one launch (start us, length us, event | category | flops | bytes accessed | tf_op | source)
XLA Modules:
  0.0 206.8 jit_solution(3272103456454151870)
XLA Ops:
  0.6 0.0 copy-start
  0.6 0.9 reshape.40
  1.5 0.7 reshape.41.mine_ref
  2.2 1.0 reshape.44
  3.2 0.3 copy.21
  3.5 0.8 copy.23.ctf_ref
  4.4 0.0 copy-done
  4.4 0.7 reshape.42
  5.0 0.2 copy.20
  5.2 1.0 copy.22.rott_ref
  6.2 29.2 %start_stage.1 = (s32[64,128]{1,0:T(8,128)}, s32[64,128]{1,0:T(8,128)}, s32[2,1024]{1,0:T(2,128)}, bf16[64,32,128]{2,1,0:T(8,128)(2,1)}, f32[8192,128]{1,0:T(8,128)}) custom-call(s32[2,1024]{1,0:T(2,128)} %bitcast.17, s32[1,1024]{1,0:T(1,128)} %bitcast.18, bf16[32,128]{1,0:T(8,128)(2,1)} %reshape.41.mine_ref, bf16[1024,1024]{1,0:T(8,128)(2,1)} %part_ref.1), custom_call_target="tpu_custom_call" | custom-call | tf_op jit(solution)/shard_map/start_stage/pallas_call | solution.py:160
  35.5 43.8 %score_stage.1 = (f32[2560,256]{1,0:T(8,128)}, bf16[64,64,1024]{2,1,0:T(8,128)(2,1)}) custom-call(s32[64,128]{1,0:T(8,128)} %get-tuple-element.16.tab_ref, f32[8192,128]{1,0:T(8,128)} %get-tuple-element.17.xs, bf16[64,32,128]{2,1,0:T(8,128)(2,1)} %get-tuple-element.18.refs_ref, bf16[256,1024]{1,0:T(8,128)(2,1)} %copy.22.rott_ref, f32[32,1024]{1,0:T(8,128)} %copy.23.ctf_ref, ...), custom_call_target="tpu_custom_call" | custom-call | tf_op jit(solution)/shard_map/score_stage/pallas_call | solution.py:269
  79.2 45.6 %soft_stage.1 = (bf16[4,640,256]{2,1,0:T(8,128)(2,1)}, f32[1,1024]{1,0:T(1,128)}) custom-call(f32[4,640,256]{2,1,0:T(8,128)} %bitcast.12, s32[2,1024]{1,0:T(2,128)} %get-tuple-element.21.rho_ref), custom_call_target="tpu_custom_call" | custom-call | tf_op jit(solution)/shard_map/soft_stage/pallas_call | solution.py:401
  124.8 0.0 copy-start.1
  124.8 33.7 %sum_stage.1 = (bf16[64,32,128]{2,1,0:T(8,128)(2,1)}, f32[64,8,256]{2,1,0:T(8,128)}) custom-call(s32[64,128]{1,0:T(8,128)} %get-tuple-element.16.tab_ref, bf16[4,640,256]{2,1,0:T(8,128)(2,1)} %get-tuple-element.22.w_ref, bf16[64,64,1024]{2,1,0:T(8,128)(2,1)} %get-tuple-element.23.weighted_ref, bf16[256,1024]{1,0:T(8,128)(2,1)} %copy.22.rott_ref, ...), custom_call_target="tpu_custom_call" | custom-call | tf_op jit(solution)/shard_map/sum_stage/pallas_call | solution.py:516
  158.4 45.0 %end_stage.1 = (bf16[64,64]{1,0:T(8,128)(2,1)}, f32[64,64]{1,0:T(8,128)}) custom-call(bf16[64,32,128]{2,1,0:T(8,128)(2,1)} %get-tuple-element.24.sums_ref, f32[64,8,256]{2,1,0:T(8,128)} %get-tuple-element.25.pk_ref, f32[32,1024]{1,0:T(8,128)} %copy.23.ctf_ref, bf16[256,1024]{1,0:T(8,128)(2,1)} %copy.22.rott_ref), custom_call_target="tpu_custom_call" | custom-call | tf_op jit(solution)/shard_map/end_stage/pallas_call | solution.py:626
  203.4 1.4 reshape.47
  204.8 1.4 reshape.48
  206.3 0.0 copy-done.1
  206.3 0.6 copy.30
  (1 shorter events, 0.0 us)
Async XLA Ops:
  0.6 3.7 %copy-start = (bf16[64,64,64]{2,1,0:T(8,128)(2,1)S(1)}, bf16[64,64,64]{2,1,0:T(8,128)(2,1)}, u32[]{:S(2)}) copy-start(bf16[64,64,64]{2,1,0:T(8,128)(2,1)} %param.11) | copy-start | bytes 1572868
  124.8 81.5 %copy-start.1 = (f32[1,1024]{1,0:T(1,128)S(1)}, f32[1,1024]{1,0:T(1,128)}, u32[]{:S(2)}) copy-start(f32[1,1024]{1,0:T(1,128)} %get-tuple-element.28) | copy-start | bytes 12292

commit v3 on v2

v3 whole, which is shorter than its diff:
```python
import functools

import jax
import jax.numpy as jnp
from jax import lax
from jax.experimental import pallas as pl
from jax.experimental.pallas import tpu as pltpu
from jax.sharding import PartitionSpec as P

F32 = jnp.float32
BF16 = jnp.bfloat16
I32 = jnp.int32
MESH = pl.DeviceIdType.MESH
NT = (((1,), (1,)), ((), ()))
NN = (((1,), (0,)), ((), ()))

GROUPS = 64
SLOTS = 64
ANG = 64
CYC = 16
CPG = 4
ROT = 64
PAIRS = CPG * ROT
PIX = CYC * ANG
KINDS = 32
TOK = 1024
SHARES = 4
ROWS = 640
PACKED = SHARES * ROWS
CHUNKS = ROWS // 64
PAIRS_OF = GROUPS // 2
Z, X = 8, 4
VMEM_LIMIT = 60 * 1024 * 1024


def mm(a, b, dims=NN):
    return lax.dot_general(a, b, dims, preferred_element_type=F32)


def iota(shape, dim):
    return lax.broadcasted_iota(I32, shape, dim)


def pieces(x):
    p1 = x.astype(BF16)
    r1 = x - p1.astype(F32)
    p2 = r1.astype(BF16)
    p3 = (r1 - p2.astype(F32)).astype(BF16)
    return p1, p2, p3


def onehot(mask):
    return jnp.where(mask, 1.0, 0.0).astype(BF16)


def vm(n):
    return [pl.BlockSpec(memory_space=pltpu.VMEM)] * n


def route(me, cand_ref, kind_ref, tab_ref, kinds_ref, rho_ref, pack_ref):
    g_iota = iota((GROUPS, TOK), 0)
    tri = onehot(iota((256, 256), 0) < iota((256, 256), 1))
    count = jnp.zeros((GROUPS, 1), F32)
    owners, ranks = [], []
    for j in range(2):
        owner = onehot(g_iota == ((cand_ref[j : j + 1, :] - me) & (GROUPS - 1)))
        owners.append(owner)
        row = []
        for blk in range(TOK // 256):
            part = owner[:, blk * 256 : (blk + 1) * 256]
            before = mm(part, tri) + count
            row.append(jnp.sum(before * part.astype(F32), axis=0, keepdims=True))
            count = count + jnp.sum(part.astype(F32), axis=1, keepdims=True)
        ranks.append(jnp.concatenate(row, axis=1))
    padded = jnp.floor((count + 7.0) * 0.125) * 8.0
    low = onehot(iota((GROUPS, GROUPS), 1) < iota((GROUPS, GROUPS), 0))
    offset = mm(low, jnp.broadcast_to(padded, (GROUPS, 128)).astype(BF16))[:, 0:1]
    at = iota((GROUPS, 384), 1) * 8
    ended = jnp.where(at >= (offset + padded).astype(I32), 1, 0)
    where_in = jnp.sum(ended, axis=0, keepdims=True)
    first = jnp.sum(jnp.where(iota((GROUPS, 384), 0) == where_in, offset.astype(I32), 0), axis=0, keepdims=True)
    source = where_in * 8 + (iota((1, 384), 1) - lax.shift_right_logical(first, 3))
    pack_ref[...] = jnp.where(where_in < GROUPS, source, 0)
    tok = iota((1, TOK), 1)
    s_iota = iota((SLOTS, TOK), 0)
    high = jnp.zeros((GROUPS, SLOTS), F32)
    low_part = jnp.zeros((GROUPS, SLOTS), F32)
    for j in range(2):
        slot = onehot(s_iota == ranks[j].astype(I32))
        v1 = (tok // 8).astype(F32)
        v2 = ((tok % 8) * 32 + kind_ref[...]).astype(F32)
        high = high + mm(owners[j], (slot.astype(F32) * v1).astype(BF16), NT)
        low_part = low_part + mm(owners[j], (slot.astype(F32) * v2).astype(BF16), NT)
        at = jnp.sum(owners[j].astype(F32) * offset, axis=0, keepdims=True) + ranks[j]
        rho_ref[j : j + 1, :] = at.astype(I32)
    low_int = low_part.astype(I32)
    kinds = low_int % 32
    token = high.astype(I32) * 8 + low_int // 32
    s_lane = iota((GROUPS, SLOTS), 1)
    live = s_lane < count.astype(I32)
    tab_ref[:, 0:SLOTS] = token + 1024 * kinds
    extra = jnp.where(s_lane == 0, offset * 0.125, count)
    tab_ref[:, SLOTS : 2 * SLOTS] = extra.astype(I32)
    kinds_ref[:, 0:SLOTS] = jnp.where(live, kinds, -1)
    kinds_ref[:, SLOTS : 2 * SLOTS] = jnp.full((GROUPS, SLOTS), -1, I32)


def turn_pixels(part_ref, xs_ref, perm, begin, end):
    def make_perm(i, _):
        r = iota((64, PIX), 0)
        c = iota((64, PIX), 1)
        hit = c == (r * CYC + i)
        perm[pl.ds(pl.multiple_of(i * 64, 64), 64), :] = onehot(hit)
        return 0

    if begin == 0:
        lax.fori_loop(0, CYC, make_perm, 0)

    def turn_rows(i, _):
        y = mm(part_ref[pl.ds(pl.multiple_of(i * 128, 128), 128), :], perm[...])
        for j in range(8):
            xs_ref[pl.ds(i * 1024 + j, 128, stride=8), :] = y[:, j * 128 : (j + 1) * 128]
        return 0

    lax.fori_loop(begin, end, turn_rows, 0)


def start_kernel(cand_ref, kind_ref, mine_ref, part_ref, tab_ref, kinds_ref, rho_ref, pack_ref, all_ref, xs_ref, perm, send_sem, recv_sem, own_sem):
    me = lax.axis_index("dom")
    row = lax.axis_index("cls")
    z, x, core = me // 8, (me // 2) % X, me % 2

    def peer(n):
        if n < 7:
            return lax.rem(z + n + 1, Z) * 8 + x * 2 + core
        if n < 10:
            return z * 8 + lax.rem(x + n - 6, X) * 2 + core
        return z * 8 + x * 2 + (1 - core)

    barrier = pltpu.get_barrier_semaphore()
    for n in range(11):
        pl.semaphore_signal(barrier, inc=1, device_id=(row, peer(n)), device_id_type=MESH)
    pl.semaphore_wait(barrier, 11)

    def copy(n):
        if n < 7:
            src, dst = mine_ref, all_ref.at[z, x, core]
        elif n < 10:
            src = dst = all_ref.at[:, x, core]
        else:
            src = dst = all_ref.at[:, :, core]
        return pltpu.make_async_remote_copy(
            src_ref=src,
            dst_ref=dst,
            send_sem=send_sem.at[n],
            recv_sem=recv_sem.at[n],
            device_id=(row, peer(n)),
            device_id_type=MESH,
        )

    first = [copy(n) for n in range(7)]
    second = [copy(n) for n in range(7, 10)]
    third = copy(10)
    for c in first:
        c.start()
    own = pltpu.make_async_copy(mine_ref, all_ref.at[z, x, core], own_sem)
    own.start()
    route(me, cand_ref, kind_ref, tab_ref, kinds_ref, rho_ref, pack_ref)
    own.wait()
    for c in first:
        c.wait()
    for c in second:
        c.start()
    turn_pixels(part_ref, xs_ref, perm, 0, 4)
    for c in second:
        c.wait()
    third.start()
    turn_pixels(part_ref, xs_ref, perm, 4, 8)
    third.wait()


def start_stage(cand_t, kinds_row, mine, particles):
    return pl.pallas_call(
        start_kernel,
        out_shape=(
            jax.ShapeDtypeStruct((GROUPS, 2 * SLOTS), I32),
            jax.ShapeDtypeStruct((GROUPS, 2 * SLOTS), I32),
            jax.ShapeDtypeStruct((2, TOK), I32),
            jax.ShapeDtypeStruct((1, 384), I32),
            jax.ShapeDtypeStruct((Z, X, 2, 32, 128), BF16),
            jax.ShapeDtypeStruct((TOK * 8, 128), F32),
        ),
        in_specs=vm(4),
        out_specs=tuple(vm(6)),
        scratch_shapes=[
            pltpu.VMEM((PIX, PIX), BF16),
            pltpu.SemaphoreType.DMA((11,)),
            pltpu.SemaphoreType.DMA((11,)),
            pltpu.SemaphoreType.DMA,
        ],
        compiler_params=pltpu.CompilerParams(collective_id=0, has_side_effects=True, vmem_limit_bytes=VMEM_LIMIT),
        name="start_stage",
    )(cand_t, kinds_row, mine, particles)


def ring_hop(ring, n, k, to, dom, src, dst):
    return pltpu.make_async_remote_copy(
        src_ref=src,
        dst_ref=dst,
        send_sem=ring.at[0, n, k],
        recv_sem=ring.at[1, n, k],
        device_id=(to, dom),
        device_id_type=MESH,
    )


def score_kernel(tab_ref, pack_ref, xs, refs_ref, rott_ref, ctf_ref, kinds_ref, total_ref, wout_ref, cs, power, bd, raw, rot_a, rot_b, stage_a, stage_b, hits_a, hits_b, wall, table, packed, far, held, near, ring, out_sem):
    rots, stages, hits = (rot_a, rot_b), (stage_a, stage_b), (hits_a, hits_b)
    me = lax.axis_index("cls")
    dom = lax.axis_index("dom")
    right, left, across = lax.rem(me + 1, SHARES), lax.rem(me + 3, SHARES), lax.rem(me + 2, SHARES)
    low, high = pl.ds(0, 32), pl.ds(32, 32)
    barrier = pltpu.get_barrier_semaphore()
    for to in (right, left):
        pl.semaphore_signal(barrier, inc=1, device_id=(to, dom), device_id_type=MESH)
    pl.semaphore_wait(barrier, 2)

    def outgoing(k):
        return (
            ring_hop(ring, 0, k, right, dom, packed.at[k, across, low], far.at[k, 0]),
            ring_hop(ring, 1, k, left, dom, packed.at[k, across, high], far.at[k, 1]),
            ring_hop(ring, 2, k, right, dom, packed.at[k, right, high], near.at[k, 0, high]),
            ring_hop(ring, 3, k, left, dom, packed.at[k, left, low], near.at[k, 1, low]),
        )

    def relayed(k):
        return (
            ring_hop(ring, 4, k, right, dom, held.at[k, 0], near.at[k, 0, low]),
            ring_hop(ring, 5, k, left, dom, held.at[k, 1], near.at[k, 1, high]),
        )

    def pack(k):
        for q in range(SHARES):
            for j in range(8):
                src = pack_ref[0, k * 32 + q * 8 + j]
                packed[k, q, j * 8 : (j + 1) * 8, :] = table[src]
        for c in outgoing(k):
            c.start()

    def relay(k):
        c0, c1, _, _ = outgoing(k)
        c0.wait()
        c1.wait()
        held[k, 0] = packed[k, right, low, :] + far[k, 0]
        held[k, 1] = packed[k, left, high, :] + far[k, 1]
        for c in relayed(k):
            c.start()

    for j in range(8):
        cs[:, j, :] = ctf_ref[:, j * 128 : (j + 1) * 128]
    square = -0.5 * (ctf_ref[...] * ctf_ref[...])
    s1 = square.astype(BF16)
    power[0:32, :] = s1
    power[32:64, :] = (square - s1.astype(F32)).astype(BF16)
    bd[...] = jnp.zeros_like(bd)
    half = iota((1, 128), 1) < 64
    keep = jnp.broadcast_to(half, (64, 128))
    keep_16 = jnp.broadcast_to(half, (16, 128))
    blank = jnp.zeros((16, 128), BF16)
    k_row = iota((128, 128), 0)

    def rotate(pair):
        for u in range(2):
            for cl in range(2):
                x = refs_ref[lax.rem(dom + pair * 2 + u, GROUPS), cl * 16 : (cl + 1) * 16, :]
                y = pltpu.roll(x, 64, 1)
                for ch, (low, high) in enumerate(((x, y), (y, x))):
                    at = u * 256 + (ch * 2 + cl) * 64
                    low = jnp.where(keep_16, low, blank)
                    high = jnp.where(keep_16, blank, high)
                    bd[at : at + 16, 0:128] = low
                    bd[at + 16 : at + 32, 0:128] = high
                    bd[at + 32 : at + 48, 128:256] = low
                    bd[at + 48 : at + 64, 128:256] = high
        for n in range(4):
            at = slice(n * 256, (n + 1) * 256)
            raw[:, at] = mm(bd[...], rott_ref[:, at]).astype(BF16)

    def arrange(pair, u):
        g = pair * 2 + u
        rot, stage = rots[u], stages[u]
        for s in range(SLOTS):
            entry = tab_ref[g, s]
            stage[s * 8 : (s + 1) * 8, :] = xs[entry & 1023] * cs[lax.shift_right_logical(entry, 10)]
        for qp in range(8):
            for k in range(2):
                r0 = u * 256 + k * 128
                a = raw[r0 : r0 + 64, qp * 128 : (qp + 1) * 128]
                b = raw[r0 + 64 : r0 + 128, qp * 128 : (qp + 1) * 128]
                rot[qp * 128 : qp * 128 + 64, k * 128 : (k + 1) * 128] = jnp.where(keep, a, pltpu.roll(b, 64, 1))
                rot[qp * 128 + 64 : qp * 128 + 128, k * 128 : (k + 1) * 128] = jnp.where(keep, pltpu.roll(a, 64, 1), b)
        for j in range(8):
            col = stage[pl.ds(j, SLOTS, stride=8), :].astype(BF16)
            wall[g, :, j * 128 : (j + 1) * 128] = col
        kinds = kinds_ref[pl.ds(g, 1), :]
        hit = jnp.where(((k_row & 31) == kinds) & (k_row < 64), 1.0, 0.0)
        hits[u][...] = jnp.transpose(hit)[0:SLOTS, :].astype(BF16)

    def score(pair, u):
        g = pair * 2 + u
        rot = rots[u]
        en, total = None, None
        for part in range(2):
            at = slice(part * 512, (part + 1) * 512)
            r = rot[at, :]
            z = mm(wall[g, :, at], r)
            y = mm(power[:, at], r * r)
            total = z if total is None else total + z
            en = y if en is None else en + y
        en = en[0:32, :] + en[32:64, :]
        p1 = en.astype(BF16)
        p2 = (en - p1.astype(F32)).astype(BF16)
        total = total + mm(hits[u][:, 0:64], jnp.concatenate([p1, p2], axis=0))
        table[pl.ds(g * 8, 8)] = (total * (4.0 / 64.0)).reshape(8, 8, PAIRS)

    def saved(g):
        return pltpu.make_async_copy(wall.at[g], wout_ref.at[g], out_sem.at[g])

    def step(t, _):
        for u in range(2):
            score(jnp.clip(t - 2, 0, PAIRS_OF - 1), u)
        for u in range(2):
            arrange(jnp.clip(t - 1, 0, PAIRS_OF - 1), u)
        rotate(jnp.minimum(t, PAIRS_OF - 1))
        return 0

    lax.fori_loop(0, 18, step, 0)

    def chunk(k, _):
        lax.fori_loop(18 + 2 * k, 20 + 2 * k, step, 0)
        pack(k)

        @pl.when(k > 0)
        def _():
            relay(k - 1)

        return 0

    lax.fori_loop(0, 8, chunk, 0)

    def save(g, _):
        saved(g).start()
        return 0

    pack(8)
    relay(7)
    pack(9)
    relay(8)
    lax.fori_loop(0, GROUPS, save, 0)
    relay(9)

    def finish(k, _):
        _, _, c2, c3 = outgoing(k)
        c4, c5 = relayed(k)
        for c in (c2, c3, c4, c5):
            c.wait()
        total_ref[k] = packed[k, me] + near[k, 0] + near[k, 1]
        return 0

    lax.fori_loop(0, CHUNKS, finish, 0)

    def save_end(g, _):
        saved(g).wait()
        return 0

    lax.fori_loop(0, GROUPS, save_end, 0)


def score_stage(tab, packing, xs, refs, rott, ctf, kinds):
    return pl.pallas_call(
        score_kernel,
        out_shape=(
            jax.ShapeDtypeStruct((CHUNKS, 64, PAIRS), F32),
            jax.ShapeDtypeStruct((GROUPS, SLOTS, PIX), BF16),
        ),
        in_specs=[pl.BlockSpec(memory_space=pltpu.SMEM)] * 2 + vm(5),
        out_specs=(pl.BlockSpec(memory_space=pltpu.VMEM), pl.BlockSpec(memory_space=pl.ANY)),
        scratch_shapes=[
            pltpu.VMEM((KINDS, 8, 128), F32),
            pltpu.VMEM((64, PIX), BF16),
            pltpu.VMEM((512, 256), BF16),
            pltpu.VMEM((512, PIX), BF16),
            pltpu.VMEM((PIX, PAIRS), BF16),
            pltpu.VMEM((PIX, PAIRS), BF16),
            pltpu.VMEM((SLOTS * 8, 128), F32),
            pltpu.VMEM((SLOTS * 8, 128), F32),
            pltpu.VMEM((SLOTS, 128), BF16),
            pltpu.VMEM((SLOTS, 128), BF16),
            pltpu.VMEM((GROUPS, SLOTS, PIX), BF16),
            pltpu.VMEM((GROUPS * 8, 8, PAIRS), F32),
            pltpu.VMEM((CHUNKS, SHARES, 64, PAIRS), F32),
            pltpu.VMEM((CHUNKS, 2, 32, PAIRS), F32),
            pltpu.VMEM((CHUNKS, 2, 32, PAIRS), F32),
            pltpu.VMEM((CHUNKS, 2, 64, PAIRS), F32),
            pltpu.SemaphoreType.DMA((2, 6, CHUNKS)),
            pltpu.SemaphoreType.DMA((GROUPS,)),
        ],
        compiler_params=pltpu.CompilerParams(collective_id=1, has_side_effects=True, vmem_limit_bytes=VMEM_LIMIT),
        name="score_stage",
    )(tab, packing, xs.reshape(TOK, 8, 128), refs.reshape(GROUPS, 32, 128), rott, ctf, kinds)


def turned(raw, rsq):
    keep = jnp.broadcast_to(iota((1, 128), 1) < 64, (64, 128))
    for qp in range(8):
        for c in range(2):
            a = raw[c * 128 : c * 128 + 64, qp * 128 : (qp + 1) * 128]
            b = raw[c * 128 + 64 : c * 128 + 128, qp * 128 : (qp + 1) * 128]
            e = jnp.where(keep, a, pltpu.roll(b, 64, 1))
            o = jnp.where(keep, pltpu.roll(a, 64, 1), b)
            rsq[qp * 128 : qp * 128 + 64, c * 128 : (c + 1) * 128] = e
            rsq[qp * 128 + 64 : qp * 128 + 128, c * 128 : (c + 1) * 128] = o


def diagonal(rott_ref, rsq):
    lane = iota((1, 256), 1)
    total = None
    for part in range(2):
        at = slice(part * 512, (part + 1) * 512)
        full = mm(rott_ref[:, at], rsq[at, :])
        diag = full[0:64, :]
        for b in range(1, 4):
            diag = jnp.where((lane // CYC) % 4 == b, full[b * 64 : (b + 1) * 64, :], diag)
        total = diag if total is None else total + diag
    return total


def folds():
    ri = iota((256, 128), 0)
    ci = iota((256, 128), 1)
    want = (ri // 64) * CYC + ri % CYC
    return [onehot(ci == want + 64 * h) for h in range(2)]


def folded(parts, fold):
    out = None
    for x, f in zip(parts, fold):
        p1 = x.astype(BF16)
        p2 = (x - p1.astype(F32)).astype(BF16)
        y = mm(p1, f) + mm(p2, f)
        out = y if out is None else out + y
    return out


def tail_kernel(tab_ref, kinds_ref, rho_ref, total_ref, rott_ref, ctf_ref, wout_ref, cs_ref, cw_ref, log_ref, weighted, w_ref, wide, stat, stat_recv, rsq_a, rsq_b, raw_a, raw_b, parts, msg, got, mine, others, ring, stat_sem, ssem, rsem, share_sem, load_sem):
    rsqs, raws = (rsq_a, rsq_b), (raw_a, raw_b)
    me = lax.axis_index("cls")
    dom = lax.axis_index("dom")
    right, left = lax.rem(me + 1, SHARES), lax.rem(me + 3, SHARES)
    low, high = pl.ds(0, 32), pl.ds(32, 32)
    load = pltpu.make_async_copy(wout_ref, weighted, load_sem)
    load.start()
    barrier = pltpu.get_barrier_semaphore()
    for d in range(1, SHARES):
        pl.semaphore_signal(barrier, inc=1, device_id=(lax.rem(me + d, SHARES), dom), device_id_type=MESH)

    def greet(i, _):
        pl.semaphore_signal(barrier, inc=1, device_id=(me, lax.rem(dom + i, GROUPS)), device_id_type=MESH)
        return 0

    lax.fori_loop(1, GROUPS, greet, 0)
    lanes = iota((64, 128), 1)
    top = jnp.zeros((64, 128), F32)
    tot = jnp.zeros((64, 128), F32)
    for k in range(CHUNKS):
        x = total_ref[k]
        m = jnp.max(x, axis=1, keepdims=True)
        s = jnp.sum(jnp.exp(x - m), axis=1, keepdims=True)
        here = lanes == 4 * k + me
        top = jnp.where(here, m, top)
        tot = jnp.where(here, s, tot)
    stat[0] = top
    stat[1] = tot
    pl.semaphore_wait(barrier, GROUPS - 1 + SHARES - 1)

    def to_peer(sem, d, src, dst):
        return pltpu.make_async_remote_copy(
            src_ref=src,
            dst_ref=dst,
            send_sem=sem.at[0, d],
            recv_sem=sem.at[1, d],
            device_id=(lax.rem(me + d, SHARES), dom),
            device_id_type=MESH,
        )

    swaps = [to_peer(stat_sem, d, stat, stat_recv.at[d - 1]) for d in (2, 1, 3)]
    for c in swaps:
        c.start()
    his, los = [], []
    for j in range(2):
        rho = rho_ref[j : j + 1, :]
        his.append(onehot(iota((128, TOK), 0) == lax.shift_right_logical(rho, 6)))
        los.append(jnp.where(iota((64, TOK), 0) == (rho & 63), 1.0, 0.0))
    for c in swaps:
        c.wait()
    top = stat[0] + stat_recv[0, 0] + stat_recv[1, 0] + stat_recv[2, 0]
    tot = stat[1] + stat_recv[0, 1] + stat_recv[1, 1] + stat_recv[2, 1]
    three = jnp.concatenate(list(pieces(top)) + list(pieces(tot)), axis=0)
    maxima, sums = [], []
    for j in range(2):
        t = mm(three, his[j])
        maxima.append(jnp.sum((t[0:64] + t[64:128] + t[128:192]) * los[j], axis=0, keepdims=True))
        sums.append(jnp.sum((t[192:256] + t[256:320] + t[320:384]) * los[j], axis=0, keepdims=True))
    best = jnp.maximum(maxima[0], maxima[1])
    log = best + jnp.log(sums[0] * jnp.exp(maxima[0] - best) + sums[1] * jnp.exp(maxima[1] - best))
    log_ref[...] = log
    back = jnp.zeros((64, 128), F32)
    for j in range(2):
        for p in pieces(log):
            back = back + mm((los[j] * p.astype(F32)).astype(BF16), his[j], NT)
    for k in range(CHUNKS):
        col = jnp.sum(jnp.where(lanes == 4 * k + me, back, 0.0), axis=1, keepdims=True)
        w_ref[k, me] = jnp.exp(total_ref[k] - col).astype(BF16)

    def own(k):
        return (
            ring_hop(ring, 0, k, right, dom, w_ref.at[k, me], w_ref.at[k, me]),
            ring_hop(ring, 1, k, left, dom, w_ref.at[k, me], w_ref.at[k, me]),
        )

    def forward(k):
        return (
            ring_hop(ring, 2, k, right, dom, w_ref.at[k, left, low], w_ref.at[k, left, low]),
            ring_hop(ring, 3, k, left, dom, w_ref.at[k, right, high], w_ref.at[k, right, high]),
        )

    def begin(copies):
        for c in copies:
            c.start()

    def end(copies):
        for c in copies:
            c.wait()

    for k in range(3):
        begin(own(k))
    end(own(0))
    begin(forward(0))
    load.wait()
    s_col = iota((SLOTS, PAIRS), 0)
    k_col = iota((8, 128), 0) + me * 8
    fold = folds()

    def spread_out(pair, u, raw):
        g = pair * 2 + u
        at = tab_ref[g, SLOTS]
        w = jnp.concatenate([wide[at + j] for j in range(8)], axis=0)
        w = jnp.where(s_col < tab_ref[g, SLOTS + 1], w, 0.0)
        wt = jnp.transpose(w).astype(BF16)
        for n in range(4):
            at = slice(n * 256, (n + 1) * 256)
            raw[:, at] = mm(wt, weighted[g, :, at]).astype(BF16)
        kinds = kinds_ref[pl.ds(g, 1), :]
        hit = onehot(k_col == kinds)[:, 0:SLOTS]
        pk = mm(hit, w.astype(BF16))
        msg[g, 32:48, :] = jnp.concatenate([pk[:, 0:128], pk[:, 128:256]], axis=0).astype(BF16)

    def fold_pair(pair):
        out = folded([parts[h] for h in range(2)], fold).astype(BF16)
        for u in range(2):
            msg[pair * 2 + u, 0:32, :] = out[u * 32 : (u + 1) * 32, :]

    def to_owner(i):
        return pltpu.make_async_remote_copy(
            src_ref=msg.at[i],
            dst_ref=got.at[i],
            send_sem=ssem.at[i],
            recv_sem=rsem.at[i],
            device_id=(me, lax.rem(dom + i, GROUPS)),
            device_id_type=MESH,
        )

    def step(t, _):
        @pl.when(t > 4)
        def _():
            to_owner(2 * (t - 4)).start()

        @pl.when(t > 3)
        def _():
            to_owner(2 * (t - 4) + 1).start()

        fold_pair(jnp.clip(t - 3, 0, PAIRS_OF - 1))
        for u in range(2):
            diag = diagonal(rott_ref, rsqs[u])
            for h in range(2):
                parts[h, u * 32 : (u + 1) * 32, :] = diag[h * 32 : (h + 1) * 32, :]
        for u in range(2):
            turned(raws[u], rsqs[u])
        for u in range(2):
            spread_out(jnp.minimum(t, PAIRS_OF - 1), u, raws[u])
        return 0

    def chunk(k, _):
        @pl.when(k + 3 < CHUNKS)
        def _():
            begin(own(k + 3))

        @pl.when(k + 1 < CHUNKS)
        def _():
            end(own(k + 1))
            begin(forward(k + 1))

        end(forward(k))
        for q in range(SHARES):
            wide[pl.ds(k * 32 + q * 8, 8)] = w_ref[k, q].astype(F32).reshape(8, 8, PAIRS)
        lax.fori_loop(2 * k, 2 * k + 2, step, 0)
        return 0

    lax.fori_loop(0, CHUNKS, chunk, 0)
    lax.fori_loop(2 * CHUNKS, PAIRS_OF + 3, step, 0)
    for u in range(2):
        to_owner(GROUPS - 2 + u).start()

    def arrive(i, acc):
        to_owner(i).wait()
        return acc + got[i].astype(F32)

    acc = lax.fori_loop(1, GROUPS, arrive, msg[0].astype(F32))
    mine[...] = acc[32:48, :]
    shares = [to_peer(share_sem, d, mine, others.at[d - 1]) for d in range(1, SHARES)]
    for c in shares:
        c.start()

    def placed(x, ref):
        t = jnp.transpose(x)
        ref[:, 0:32] = t[0:64, :].astype(ref.dtype)
        ref[:, 32:64] = t[64:128, :].astype(ref.dtype)

    placed(acc[0:32, :], cs_ref)
    for c in shares:
        c.wait()
    rows = []
    for k in range(SHARES):
        x = mine[...]
        for d in range(1, SHARES):
            x = jnp.where(lax.rem(k + d, SHARES) == me, others[d - 1], x)
        rows.append(jnp.concatenate([x[0:8, :], x[8:16, :]], axis=1))
    pkt = jnp.transpose(jnp.concatenate(rows, axis=0))
    power = ctf_ref[...] * ctf_ref[...]
    for n in range(4):
        at = slice(n * 256, (n + 1) * 256)
        raw_a[:, at] = lax.dot_general(
            pkt, power[:, at], NN, precision=lax.Precision.HIGHEST, preferred_element_type=F32
        ).astype(BF16)
    turned(raw_a, rsq_a)
    diag = diagonal(rott_ref, rsq_a)
    placed(folded([diag[0:32], diag[32:64]], folds()), cw_ref)


def tail_stage(tab, kinds, rho, total, rott, ctf, weighted):
    return pl.pallas_call(
        tail_kernel,
        out_shape=(
            jax.ShapeDtypeStruct((64, 64), BF16),
            jax.ShapeDtypeStruct((64, 64), F32),
            jax.ShapeDtypeStruct((1, TOK), F32),
        ),
        in_specs=[pl.BlockSpec(memory_space=pltpu.SMEM)] + vm(5) + [pl.BlockSpec(memory_space=pl.ANY)],
        out_specs=tuple(vm(3)),
        scratch_shapes=[
            pltpu.VMEM((GROUPS, SLOTS, PIX), BF16),
            pltpu.VMEM((CHUNKS, SHARES, 64, PAIRS), BF16),
            pltpu.VMEM((PACKED // 8, 8, PAIRS), F32),
            pltpu.VMEM((2, 64, 128), F32),
            pltpu.VMEM((SHARES - 1, 2, 64, 128), F32),
            pltpu.VMEM((1024, 256), BF16),
            pltpu.VMEM((1024, 256), BF16),
            pltpu.VMEM((PAIRS, PIX), BF16),
            pltpu.VMEM((PAIRS, PIX), BF16),
            pltpu.VMEM((2, 64, 256), F32),
            pltpu.VMEM((GROUPS, 48, 128), BF16),
            pltpu.VMEM((GROUPS, 48, 128), BF16),
            pltpu.VMEM((16, 128), F32),
            pltpu.VMEM((SHARES - 1, 16, 128), F32),
            pltpu.SemaphoreType.DMA((2, 4, CHUNKS)),
            pltpu.SemaphoreType.DMA((2, SHARES)),
            pltpu.SemaphoreType.DMA((GROUPS,)),
            pltpu.SemaphoreType.DMA((GROUPS,)),
            pltpu.SemaphoreType.DMA((2, SHARES)),
            pltpu.SemaphoreType.DMA,
        ],
        compiler_params=pltpu.CompilerParams(collective_id=2, has_side_effects=True, vmem_limit_bytes=VMEM_LIMIT),
        name="tail_stage",
    )(tab, kinds, rho, total, rott, ctf, weighted)


def prepared(candidates, defocus, ctf_table, references, rotations):
    mine = references.reshape(2, 2, CYC, ANG).transpose(1, 2, 0, 3).reshape(32, 128)
    rott = rotations.reshape(ROT, CYC, 4 * ANG).transpose(2, 1, 0).reshape(256, 1024)
    ctf = ctf_table.reshape(KINDS, CYC, ANG).transpose(0, 2, 1).reshape(KINDS, PIX)
    return mine, rott, ctf, candidates.T, defocus.reshape(1, TOK)


def local(particles, candidates, defocus, ctf_table, references, rotations):
    mine, rott, ctf, cand_t, kinds_row = prepared(candidates, defocus, ctf_table, references, rotations)
    tab, kinds, rho, packing, refs, xs = start_stage(cand_t, kinds_row, mine, particles)
    total, weighted = score_stage(tab, packing, xs, refs, rott, ctf, kinds)
    cs, cw, log = tail_stage(tab, kinds, rho, total, rott, ctf, weighted)
    return cs.reshape(CPG, PIX), cw.reshape(CPG, PIX), log.reshape(TOK)


def solution(mesh):
    in_specs = (P("dom", "cls"), P("dom", None), P("dom"), P(None, "cls"), P("dom", "cls"), P())
    out_specs = (P("dom", "cls"), P("dom", "cls"), P("dom"))
    return jax.shard_map(local, mesh=mesh, in_specs=in_specs, out_specs=out_specs, check_vma=False)
```

time: 208 us -> 170 us (0.82)
  Pallas kernels: 197 us -> 158 us
    pallas_call x4 -> x2, Pallas kernels: 168 us -> 135 us  [the longest x1 71.7 us: tail_stage(): pl.pallas_call(tail_kernel, out_shape=(jax.ShapeDtypeStruct((64, 64), BF1...]
    pallas_call x1, Pallas kernels: 29.2 us -> 23.5 us  [start_stage(): pl.pallas_call(start_kernel, out_shape=(jax.ShapeDtypeStruct((GROUPS, 2 *...]
where the time goes in v3:
time: 170 us
  Pallas kernels  158 us (93%)
  local copies, waits for them, and re-layouts  10.9 us (6%)
    pallas_call x1, Pallas kernels, tail_stage(): pl.pallas_call(tail_kernel, out_shape=(jax.ShapeDtypeStruct((64, 64), BF1...  71.7 us
    pallas_call x1, Pallas kernels, score_stage(): pl.pallas_call(score_kernel, out_shape=(jax.ShapeDtypeStruct((CHUNKS, 64,...  63.1 us
    pallas_call x1, Pallas kernels, start_stage(): pl.pallas_call(start_kernel, out_shape=(jax.ShapeDtypeStruct((GROUPS, 2 *...  23.5 us

profile of v3, /device:TPU:1, one launch (start us, length us, event | category | flops | bytes accessed | tf_op | source)
XLA Modules:
  0.0 169.9 jit_solution(4485998733004975310)
XLA Ops:
  0.6 0.8 reshape.43
  1.4 0.7 reshape.44.mine_ref
  2.1 1.0 reshape.49
  3.1 0.3 copy.20
  3.4 0.8 copy.22.ctf_ref
  4.3 1.9 %reshape.47 = bf16[64,16,256]{2,1,0:T(8,128)(2,1)S(1)} reshape(bf16[64,64,64]{2,1,0:T(8,128)(2,1)} %param.11) | data formatting | bytes 1048576 | tf_op jit(solution)/shard_map/reshape | solution.py:699
  6.2 0.2 copy.19
  6.4 1.0 copy.21.rott_ref
  7.4 23.5 %start_stage.1 = (s32[64,128]{1,0:T(8,128)}, s32[64,128]{1,0:T(8,128)}, s32[2,1024]{1,0:T(2,128)}, s32[1,384]{1,0:T(1,128)}, bf16[8,4,2,32,128]{4,3,2,1,0:T(8,128)(2,1)}, /*index=5*/f32[8192,128]{1,0:T(8,128)}) custom-call(s32[2,1024]{1,0:T(2,128)} %bitcast.19, s32[1,1024]{1,0:T(1,128)} %bitcast.20, bf16[32,128]{1,0:T(8,128)(2,1)} %reshape.44.mine_ref, ...), custom_call_target="tpu_custom_call" | custom-call | tf_op jit(solution)/shard_map/start_stage/pallas_call | solution.py:183
  31.0 63.1 %score_stage.1 = (f32[10,64,256]{2,1,0:T(8,128)}, bf16[64,64,1024]{2,1,0:T(8,128)(2,1)}) custom-call(s32[64,128]{1,0:T(8,128)} %get-tuple-element.14.tab_ref, s32[1,384]{1,0:T(1,128)} %get-tuple-element.17.pack_ref, f32[1024,8,128]{2,1,0:T(8,128)} %bitcast.13, bf16[64,32,128]{2,1,0:T(8,128)(2,1)} %bitcast.17, bf16[256,1024]{1,0:T(8,128)(2,1)} %copy.21.rott_ref, ...), custom_call_target="tpu_custom_call" | custom-call | tf_op jit(solution)/shard_map/score_stage/pallas_call | solution.py:380
  94.0 71.7 %tail_stage.1 = (bf16[64,64]{1,0:T(8,128)(2,1)}, f32[64,64]{1,0:T(8,128)}, f32[1,1024]{1,0:T(1,128)}) custom-call(s32[64,128]{1,0:T(8,128)} %get-tuple-element.14.tab_ref, s32[64,128]{1,0:T(8,128)} %get-tuple-element.15.kinds_ref, s32[2,1024]{1,0:T(2,128)} %get-tuple-element.16.rho_ref, f32[10,64,256]{2,1,0:T(8,128)} %get-tuple-element.20.total_ref, ...), custom_call_target="tpu_custom_call" | custom-call | tf_op jit(solution)/shard_map/tail_stage/pallas_call | solution.py:661
  165.7 1.4 reshape.51
  167.1 1.4 reshape.52
  168.6 1.3 copy.28
  (1 shorter events, 0.0 us)

commit v4 on v3

--- a/solution.py
+++ b/solution.py
@@ -53,6 +53,10 @@
     return jnp.where(mask, 1.0, 0.0).astype(BF16)
 
 
+def owner_of(dom, i):
+    return lax.rem(dom + (i % 8) * 8 + i // 8, GROUPS)
+
+
 def vm(n):
     return [pl.BlockSpec(memory_space=pltpu.VMEM)] * n
 
@@ -63,7 +67,8 @@
     count = jnp.zeros((GROUPS, 1), F32)
     owners, ranks = [], []
     for j in range(2):
-        owner = onehot(g_iota == ((cand_ref[j : j + 1, :] - me) & (GROUPS - 1)))
+        shift = (cand_ref[j : j + 1, :] - me) & (GROUPS - 1)
+        owner = onehot(g_iota == ((shift & 7) * 8 + lax.shift_right_logical(shift, 3)))
         owners.append(owner)
         row = []
         for blk in range(TOK // 256):
@@ -203,6 +208,48 @@
     )(cand_t, kinds_row, mine, particles)
 
 
+def turned(raw, rsq):
+    keep = jnp.broadcast_to(iota((1, 128), 1) < 64, (64, 128))
+    for qp in range(8):
+        for c in range(2):
+            a = raw[c * 128 : c * 128 + 64, qp * 128 : (qp + 1) * 128]
+            b = raw[c * 128 + 64 : c * 128 + 128, qp * 128 : (qp + 1) * 128]
+            e = jnp.where(keep, a, pltpu.roll(b, 64, 1))
+            o = jnp.where(keep, pltpu.roll(a, 64, 1), b)
+            rsq[qp * 128 : qp * 128 + 64, c * 128 : (c + 1) * 128] = e
+            rsq[qp * 128 + 64 : qp * 128 + 128, c * 128 : (c + 1) * 128] = o
+
+
+def diagonal(rott_ref, rsq):
+    lane = iota((1, 256), 1)
+    total = None
+    for part in range(2):
+        at = slice(part * 512, (part + 1) * 512)
+        full = mm(rott_ref[:, at], rsq[at, :])
+        diag = full[0:64, :]
+        for b in range(1, 4):
+            diag = jnp.where((lane // CYC) % 4 == b, full[b * 64 : (b + 1) * 64, :], diag)
+        total = diag if total is None else total + diag
+    return total
+
+
+def folds():
+    ri = iota((256, 128), 0)
+    ci = iota((256, 128), 1)
+    want = (ri // 64) * CYC + ri % CYC
+    return [onehot(ci == want + 64 * h) for h in range(2)]
+
+
+def folded(parts, fold):
+    out = None
+    for x, f in zip(parts, fold):
+        p1 = x.astype(BF16)
+        p2 = (x - p1.astype(F32)).astype(BF16)
+        y = mm(p1, f) + mm(p2, f)
+        out = y if out is None else out + y
+    return out
+
+
 def ring_hop(ring, n, k, to, dom, src, dst):
     return pltpu.make_async_remote_copy(
         src_ref=src,
@@ -214,16 +261,22 @@
     )
 
 
-def score_kernel(tab_ref, pack_ref, xs, refs_ref, rott_ref, ctf_ref, kinds_ref, total_ref, wout_ref, cs, power, bd, raw, rot_a, rot_b, stage_a, stage_b, hits_a, hits_b, wall, table, packed, far, held, near, ring, out_sem):
+def main_kernel(tab_ref, pack_ref, xs, refs_ref, rott_ref, ctf_ref, kinds_ref, rho_ref, sums_ref, pk_ref, log_ref, cs, power, bd, raw, rot_a, rot_b, stage_a, stage_b, hits_a, hits_b, wall, table, packed, far, held, near, total_ref, w_ref, wide, stat, stat_recv, rsq_a, rsq_b, raw_a, raw_b, parts, msg, got, mine, others, ring, ring2, stat_sem, ssem, rsem, share_sem):
     rots, stages, hits = (rot_a, rot_b), (stage_a, stage_b), (hits_a, hits_b)
+    rsqs, raws = (rsq_a, rsq_b), (raw_a, raw_b)
     me = lax.axis_index("cls")
     dom = lax.axis_index("dom")
     right, left, across = lax.rem(me + 1, SHARES), lax.rem(me + 3, SHARES), lax.rem(me + 2, SHARES)
     low, high = pl.ds(0, 32), pl.ds(32, 32)
     barrier = pltpu.get_barrier_semaphore()
-    for to in (right, left):
-        pl.semaphore_signal(barrier, inc=1, device_id=(to, dom), device_id_type=MESH)
-    pl.semaphore_wait(barrier, 2)
+    for d in range(1, SHARES):
+        pl.semaphore_signal(barrier, inc=1, device_id=(lax.rem(me + d, SHARES), dom), device_id_type=MESH)
+
+    def greet(i, _):
+        pl.semaphore_signal(barrier, inc=1, device_id=(me, lax.rem(dom + i, GROUPS)), device_id_type=MESH)
+        return 0
+
+    lax.fori_loop(1, GROUPS, greet, 0)
 
     def outgoing(k):
         return (
@@ -272,7 +325,7 @@
     def rotate(pair):
         for u in range(2):
             for cl in range(2):
-                x = refs_ref[lax.rem(dom + pair * 2 + u, GROUPS), cl * 16 : (cl + 1) * 16, :]
+                x = refs_ref[owner_of(dom, pair * 2 + u), cl * 16 : (cl + 1) * 16, :]
                 y = pltpu.roll(x, 64, 1)
                 for ch, (low, high) in enumerate(((x, y), (y, x))):
                     at = u * 256 + (ch * 2 + cl) * 64
@@ -323,9 +376,6 @@
         total = total + mm(hits[u][:, 0:64], jnp.concatenate([p1, p2], axis=0))
         table[pl.ds(g * 8, 8)] = (total * (4.0 / 64.0)).reshape(8, 8, PAIRS)
 
-    def saved(g):
-        return pltpu.make_async_copy(wall.at[g], wout_ref.at[g], out_sem.at[g])
-
     def step(t, _):
         for u in range(2):
             score(jnp.clip(t - 2, 0, PAIRS_OF - 1), u)
@@ -335,6 +385,7 @@
         return 0
 
     lax.fori_loop(0, 18, step, 0)
+    pl.semaphore_wait(barrier, GROUPS - 1 + SHARES - 1)
 
     def chunk(k, _):
         lax.fori_loop(18 + 2 * k, 20 + 2 * k, step, 0)
@@ -347,16 +398,11 @@
         return 0
 
     lax.fori_loop(0, 8, chunk, 0)
-
-    def save(g, _):
-        saved(g).start()
-        return 0
 
     pack(8)
     relay(7)
     pack(9)
     relay(8)
-    lax.fori_loop(0, GROUPS, save, 0)
     relay(9)
 
     def finish(k, _):
@@ -369,106 +415,6 @@
 
     lax.fori_loop(0, CHUNKS, finish, 0)
 
-    def save_end(g, _):
-        saved(g).wait()
-        return 0
-
-    lax.fori_loop(0, GROUPS, save_end, 0)
-
-
-def score_stage(tab, packing, xs, refs, rott, ctf, kinds):
-    return pl.pallas_call(
-        score_kernel,
-        out_shape=(
-            jax.ShapeDtypeStruct((CHUNKS, 64, PAIRS), F32),
-            jax.ShapeDtypeStruct((GROUPS, SLOTS, PIX), BF16),
-        ),
-        in_specs=[pl.BlockSpec(memory_space=pltpu.SMEM)] * 2 + vm(5),
-        out_specs=(pl.BlockSpec(memory_space=pltpu.VMEM), pl.BlockSpec(memory_space=pl.ANY)),
-        scratch_shapes=[
-            pltpu.VMEM((KINDS, 8, 128), F32),
-            pltpu.VMEM((64, PIX), BF16),
-            pltpu.VMEM((512, 256), BF16),
-            pltpu.VMEM((512, PIX), BF16),
-            pltpu.VMEM((PIX, PAIRS), BF16),
-            pltpu.VMEM((PIX, PAIRS), BF16),
-            pltpu.VMEM((SLOTS * 8, 128), F32),
-            pltpu.VMEM((SLOTS * 8, 128), F32),
-            pltpu.VMEM((SLOTS, 128), BF16),
-            pltpu.VMEM((SLOTS, 128), BF16),
-            pltpu.VMEM((GROUPS, SLOTS, PIX), BF16),
-            pltpu.VMEM((GROUPS * 8, 8, PAIRS), F32),
-            pltpu.VMEM((CHUNKS, SHARES, 64, PAIRS), F32),
-            pltpu.VMEM((CHUNKS, 2, 32, PAIRS), F32),
-            pltpu.VMEM((CHUNKS, 2, 32, PAIRS), F32),
-            pltpu.VMEM((CHUNKS, 2, 64, PAIRS), F32),
-            pltpu.SemaphoreType.DMA((2, 6, CHUNKS)),
-            pltpu.SemaphoreType.DMA((GROUPS,)),
-        ],
-        compiler_params=pltpu.CompilerParams(collective_id=1, has_side_effects=True, vmem_limit_bytes=VMEM_LIMIT),
-        name="score_stage",
-    )(tab, packing, xs.reshape(TOK, 8, 128), refs.reshape(GROUPS, 32, 128), rott, ctf, kinds)
-
-
-def turned(raw, rsq):
-    keep = jnp.broadcast_to(iota((1, 128), 1) < 64, (64, 128))
-    for qp in range(8):
-        for c in range(2):
-            a = raw[c * 128 : c * 128 + 64, qp * 128 : (qp + 1) * 128]
-            b = raw[c * 128 + 64 : c * 128 + 128, qp * 128 : (qp + 1) * 128]
-            e = jnp.where(keep, a, pltpu.roll(b, 64, 1))
-            o = jnp.where(keep, pltpu.roll(a, 64, 1), b)
-            rsq[qp * 128 : qp * 128 + 64, c * 128 : (c + 1) * 128] = e
-            rsq[qp * 128 + 64 : qp * 128 + 128, c * 128 : (c + 1) * 128] = o
-
-
-def diagonal(rott_ref, rsq):
-    lane = iota((1, 256), 1)
-    total = None
-    for part in range(2):
-        at = slice(part * 512, (part + 1) * 512)
-        full = mm(rott_ref[:, at], rsq[at, :])
-        diag = full[0:64, :]
-        for b in range(1, 4):
-            diag = jnp.where((lane // CYC) % 4 == b, full[b * 64 : (b + 1) * 64, :], diag)
-        total = diag if total is None else total + diag
-    return total
-
-
-def folds():
-    ri = iota((256, 128), 0)
-    ci = iota((256, 128), 1)
-    want = (ri // 64) * CYC + ri % CYC
-    return [onehot(ci == want + 64 * h) for h in range(2)]
-
-
-def folded(parts, fold):
-    out = None
-    for x, f in zip(parts, fold):
-        p1 = x.astype(BF16)
-        p2 = (x - p1.astype(F32)).astype(BF16)
-        y = mm(p1, f) + mm(p2, f)
-        out = y if out is None else out + y
-    return out
-
-
-def tail_kernel(tab_ref, kinds_ref, rho_ref, total_ref, rott_ref, ctf_ref, wout_ref, cs_ref, cw_ref, log_ref, weighted, w_ref, wide, stat, stat_recv, rsq_a, rsq_b, raw_a, raw_b, parts, msg, got, mine, others, ring, stat_sem, ssem, rsem, share_sem, load_sem):
-    rsqs, raws = (rsq_a, rsq_b), (raw_a, raw_b)
-    me = lax.axis_index("cls")
-    dom = lax.axis_index("dom")
-    right, left = lax.rem(me + 1, SHARES), lax.rem(me + 3, SHARES)
-    low, high = pl.ds(0, 32), pl.ds(32, 32)
-    load = pltpu.make_async_copy(wout_ref, weighted, load_sem)
-    load.start()
-    barrier = pltpu.get_barrier_semaphore()
-    for d in range(1, SHARES):
-        pl.semaphore_signal(barrier, inc=1, device_id=(lax.rem(me + d, SHARES), dom), device_id_type=MESH)
-
-    def greet(i, _):
-        pl.semaphore_signal(barrier, inc=1, device_id=(me, lax.rem(dom + i, GROUPS)), device_id_type=MESH)
-        return 0
-
-    lax.fori_loop(1, GROUPS, greet, 0)
     lanes = iota((64, 128), 1)
     top = jnp.zeros((64, 128), F32)
     tot = jnp.zeros((64, 128), F32)
@@ -481,8 +427,6 @@
         tot = jnp.where(here, s, tot)
     stat[0] = top
     stat[1] = tot
-    pl.semaphore_wait(barrier, GROUPS - 1 + SHARES - 1)
-
     def to_peer(sem, d, src, dst):
         return pltpu.make_async_remote_copy(
             src_ref=src,
@@ -524,14 +468,14 @@
 
     def own(k):
         return (
-            ring_hop(ring, 0, k, right, dom, w_ref.at[k, me], w_ref.at[k, me]),
-            ring_hop(ring, 1, k, left, dom, w_ref.at[k, me], w_ref.at[k, me]),
+            ring_hop(ring2, 0, k, right, dom, w_ref.at[k, me], w_ref.at[k, me]),
+            ring_hop(ring2, 1, k, left, dom, w_ref.at[k, me], w_ref.at[k, me]),
         )
 
     def forward(k):
         return (
-            ring_hop(ring, 2, k, right, dom, w_ref.at[k, left, low], w_ref.at[k, left, low]),
-            ring_hop(ring, 3, k, left, dom, w_ref.at[k, right, high], w_ref.at[k, right, high]),
+            ring_hop(ring2, 2, k, right, dom, w_ref.at[k, left, low], w_ref.at[k, left, low]),
+            ring_hop(ring2, 3, k, left, dom, w_ref.at[k, right, high], w_ref.at[k, right, high]),
         )
 
     def begin(copies):
@@ -546,7 +490,6 @@
         begin(own(k))
     end(own(0))
     begin(forward(0))
-    load.wait()
     s_col = iota((SLOTS, PAIRS), 0)
     k_col = iota((8, 128), 0) + me * 8
     fold = folds()
@@ -559,7 +502,7 @@
         wt = jnp.transpose(w).astype(BF16)
         for n in range(4):
             at = slice(n * 256, (n + 1) * 256)
-            raw[:, at] = mm(wt, weighted[g, :, at]).astype(BF16)
+            raw[:, at] = mm(wt, wall[g, :, at]).astype(BF16)
         kinds = kinds_ref[pl.ds(g, 1), :]
         hit = onehot(k_col == kinds)[:, 0:SLOTS]
         pk = mm(hit, w.astype(BF16))
@@ -576,7 +519,7 @@
             dst_ref=got.at[i],
             send_sem=ssem.at[i],
             recv_sem=rsem.at[i],
-            device_id=(me, lax.rem(dom + i, GROUPS)),
+            device_id=(me, owner_of(dom, i)),
             device_id_type=MESH,
         )
 
@@ -631,12 +574,7 @@
     for c in shares:
         c.start()
 
-    def placed(x, ref):
-        t = jnp.transpose(x)
-        ref[:, 0:32] = t[0:64, :].astype(ref.dtype)
-        ref[:, 32:64] = t[64:128, :].astype(ref.dtype)
-
-    placed(acc[0:32, :], cs_ref)
+    sums_ref[...] = acc[0:32, :]
     for c in shares:
         c.wait()
     rows = []
@@ -645,30 +583,79 @@
         for d in range(1, SHARES):
             x = jnp.where(lax.rem(k + d, SHARES) == me, others[d - 1], x)
         rows.append(jnp.concatenate([x[0:8, :], x[8:16, :]], axis=1))
-    pkt = jnp.transpose(jnp.concatenate(rows, axis=0))
+    pk_ref[...] = jnp.concatenate(rows, axis=0)
+
+
+def last_kernel(sums_ref, pk_ref, log_in, ctf_ref, rott_ref, cs_ref, cw_ref, log_ref, raw, rsq, placing):
+    def placed(x, ref):
+        placing[:, 0:32] = jnp.transpose(x)
+        for l in range(CYC):
+            piece = [placing[pl.ds(h * 64 + l, CPG, stride=CYC), 0:32] for h in range(2)]
+            ref[:, l * ANG : (l + 1) * ANG] = jnp.concatenate(piece, axis=1).astype(ref.dtype)
+
+    for j in range(8):
+        log_ref[j : j + 1, :] = log_in[:, j * 128 : (j + 1) * 128]
+    placed(sums_ref[...], cs_ref)
+    pkt = jnp.transpose(pk_ref[...])
     power = ctf_ref[...] * ctf_ref[...]
     for n in range(4):
         at = slice(n * 256, (n + 1) * 256)
-        raw_a[:, at] = lax.dot_general(
+        raw[:, at] = lax.dot_general(
             pkt, power[:, at], NN, precision=lax.Precision.HIGHEST, preferred_element_type=F32
         ).astype(BF16)
-    turned(raw_a, rsq_a)
-    diag = diagonal(rott_ref, rsq_a)
+    turned(raw, rsq)
+    diag = diagonal(rott_ref, rsq)
     placed(folded([diag[0:32], diag[32:64]], folds()), cw_ref)
 
 
-def tail_stage(tab, kinds, rho, total, rott, ctf, weighted):
+def last_stage(sums, pk, log, ctf, rott):
     return pl.pallas_call(
-        tail_kernel,
+        last_kernel,
         out_shape=(
-            jax.ShapeDtypeStruct((64, 64), BF16),
-            jax.ShapeDtypeStruct((64, 64), F32),
+            jax.ShapeDtypeStruct((CPG, PIX), BF16),
+            jax.ShapeDtypeStruct((CPG, PIX), F32),
+            jax.ShapeDtypeStruct((8, TOK // 8), F32),
+        ),
+        in_specs=vm(5),
+        out_specs=tuple(vm(3)),
+        scratch_shapes=[
+            pltpu.VMEM((PAIRS, PIX), BF16),
+            pltpu.VMEM((1024, 256), BF16),
+            pltpu.VMEM((128, 128), F32),
+        ],
+        compiler_params=pltpu.CompilerParams(vmem_limit_bytes=VMEM_LIMIT),
+        name="last_stage",
+    )(sums, pk, log, ctf, rott)
+
+
+def main_stage(tab, packing, xs, refs, rott, ctf, kinds, rho):
+    return pl.pallas_call(
+        main_kernel,
+        out_shape=(
+            jax.ShapeDtypeStruct((32, 128), F32),
+            jax.ShapeDtypeStruct((KINDS, PAIRS), F32),
             jax.ShapeDtypeStruct((1, TOK), F32),
         ),
-        in_specs=[pl.BlockSpec(memory_space=pltpu.SMEM)] + vm(5) + [pl.BlockSpec(memory_space=pl.ANY)],
+        in_specs=[pl.BlockSpec(memory_space=pltpu.SMEM)] * 2 + vm(6),
         out_specs=tuple(vm(3)),
         scratch_shapes=[
+            pltpu.VMEM((KINDS, 8, 128), F32),
+            pltpu.VMEM((64, PIX), BF16),
+            pltpu.VMEM((512, 256), BF16),
+            pltpu.VMEM((512, PIX), BF16),
+            pltpu.VMEM((PIX, PAIRS), BF16),
+            pltpu.VMEM((PIX, PAIRS), BF16),
+            pltpu.VMEM((SLOTS * 8, 128), F32),
+            pltpu.VMEM((SLOTS * 8, 128), F32),
+            pltpu.VMEM((SLOTS, 128), BF16),
+            pltpu.VMEM((SLOTS, 128), BF16),
             pltpu.VMEM((GROUPS, SLOTS, PIX), BF16),
+            pltpu.VMEM((GROUPS * 8, 8, PAIRS), F32),
+            pltpu.VMEM((CHUNKS, SHARES, 64, PAIRS), F32),
+            pltpu.VMEM((CHUNKS, 2, 32, PAIRS), F32),
+            pltpu.VMEM((CHUNKS, 2, 32, PAIRS), F32),
+            pltpu.VMEM((CHUNKS, 2, 64, PAIRS), F32),
+            pltpu.VMEM((CHUNKS, 64, PAIRS), F32),
             pltpu.VMEM((CHUNKS, SHARES, 64, PAIRS), BF16),
             pltpu.VMEM((PACKED // 8, 8, PAIRS), F32),
             pltpu.VMEM((2, 64, 128), F32),
@@ -682,16 +669,16 @@
             pltpu.VMEM((GROUPS, 48, 128), BF16),
             pltpu.VMEM((16, 128), F32),
             pltpu.VMEM((SHARES - 1, 16, 128), F32),
+            pltpu.SemaphoreType.DMA((2, 6, CHUNKS)),
             pltpu.SemaphoreType.DMA((2, 4, CHUNKS)),
             pltpu.SemaphoreType.DMA((2, SHARES)),
             pltpu.SemaphoreType.DMA((GROUPS,)),
             pltpu.SemaphoreType.DMA((GROUPS,)),
             pltpu.SemaphoreType.DMA((2, SHARES)),
-            pltpu.SemaphoreType.DMA,
         ],
-        compiler_params=pltpu.CompilerParams(collective_id=2, has_side_effects=True, vmem_limit_bytes=VMEM_LIMIT),
-        name="tail_stage",
-    )(tab, kinds, rho, total, rott, ctf, weighted)
+        compiler_params=pltpu.CompilerParams(collective_id=1, has_side_effects=True, vmem_limit_bytes=VMEM_LIMIT),
+        name="main_stage",
+    )(tab, packing, xs.reshape(TOK, 8, 128), refs.reshape(GROUPS, 32, 128), rott, ctf, kinds, rho)
 
 
 def prepared(candidates, defocus, ctf_table, references, rotations):
@@ -704,9 +691,9 @@
 def local(particles, candidates, defocus, ctf_table, references, rotations):
     mine, rott, ctf, cand_t, kinds_row = prepared(candidates, defocus, ctf_table, references, rotations)
     tab, kinds, rho, packing, refs, xs = start_stage(cand_t, kinds_row, mine, particles)
-    total, weighted = score_stage(tab, packing, xs, refs, rott, ctf, kinds)
-    cs, cw, log = tail_stage(tab, kinds, rho, total, rott, ctf, weighted)
-    return cs.reshape(CPG, PIX), cw.reshape(CPG, PIX), log.reshape(TOK)
+    sums, pk, log = main_stage(tab, packing, xs, refs, rott, ctf, kinds, rho)
+    cs, cw, log = last_stage(sums, pk, log, ctf, rott)
+    return cs, cw, log.reshape(TOK)
 
 
 def solution(mesh):

time: 170 us -> 159 us (0.935)
  Pallas kernels: 158 us -> 151 us
  local copies, waits for them, and re-layouts: 10.9 us -> 6.71 us
    pallas_call x2, Pallas kernels: 135 us -> 128 us  [the longest x1 124 us: main_stage(): pl.pallas_call(main_kernel, out_shape=(jax.ShapeDtypeStruct((32, 128), F3...]
    reshape x2 -> x0, local copies, waits for them, and re-layouts: 2.85 us -> none  [local(): return (cs.reshape(CPG, PIX), cw.reshape(CPG, PIX), log.reshape(TOK))]
where the time goes in v4:
time: 159 us; the launch traced here: 158 us
  Pallas kernels  151 us (95%)
  local copies, waits for them, and re-layouts  6.71 us (4%)
    pallas_call x1, Pallas kernels, main_stage(): pl.pallas_call(main_kernel, out_shape=(jax.ShapeDtypeStruct((32, 128), F3...  124 us
    pallas_call x1, Pallas kernels, start_stage(): pl.pallas_call(start_kernel, out_shape=(jax.ShapeDtypeStruct((GROUPS, 2 *...  23.5 us
    pallas_call x1, Pallas kernels, last_stage(): pl.pallas_call(last_kernel, out_shape=(jax.ShapeDtypeStruct((CPG, PIX), B...  3.63 us

profile of v4, /device:TPU:1, one launch (start us, length us, event | category | flops | bytes accessed | tf_op | source)
XLA Modules:
  0.0 158.4 jit_solution(4280693190774900957)
XLA Ops:
  0.6 0.8 reshape.37
  1.4 0.7 reshape.38.mine_ref
  2.1 1.0 reshape.43
  3.1 0.3 copy.20
  3.4 0.8 copy.22.ctf_ref
  4.3 1.9 %reshape.41 = bf16[64,16,256]{2,1,0:T(8,128)(2,1)S(1)} reshape(bf16[64,64,64]{2,1,0:T(8,128)(2,1)} %param.11) | data formatting | bytes 1048576 | tf_op jit(solution)/shard_map/reshape | solution.py:686
  6.2 0.2 copy.19
  6.4 1.0 copy.21.rott_ref
  7.4 23.5 %start_stage.1 = (s32[64,128]{1,0:T(8,128)}, s32[64,128]{1,0:T(8,128)}, s32[2,1024]{1,0:T(2,128)}, s32[1,384]{1,0:T(1,128)}, bf16[8,4,2,32,128]{4,3,2,1,0:T(8,128)(2,1)}, /*index=5*/f32[8192,128]{1,0:T(8,128)}) custom-call(s32[2,1024]{1,0:T(2,128)} %bitcast.19, s32[1,1024]{1,0:T(1,128)} %bitcast.20, bf16[32,128]{1,0:T(8,128)(2,1)} %reshape.38.mine_ref, ...), custom_call_target="tpu_custom_call" | custom-call | tf_op jit(solution)/shard_map/start_stage/pallas_call | solution.py:188
  30.9 123.9 %main_stage.1 = (f32[32,128]{1,0:T(8,128)}, f32[32,256]{1,0:T(8,128)}, f32[1,1024]{1,0:T(1,128)}) custom-call(s32[64,128]{1,0:T(8,128)} %get-tuple-element.15.tab_ref, s32[1,384]{1,0:T(1,128)} %get-tuple-element.16.pack_ref, f32[1024,8,128]{2,1,0:T(8,128)} %bitcast.13, bf16[64,32,128]{2,1,0:T(8,128)(2,1)} %bitcast.17, bf16[256,1024]{1,0:T(8,128)(2,1)} %copy.21.rott_ref, ...), custom_call_target="tpu_custom_call" | custom-call | tf_op jit(solution)/shard_map/main_stage/pallas_call | solution.py:632
  154.8 3.6 %last_stage.1 = (bf16[4,1024]{1,0:T(4,128)(2,1)}, f32[4,1024]{1,0:T(4,128)}, f32[8,128]{1,0:T(8,128)}) custom-call(f32[32,128]{1,0:T(8,128)} %get-tuple-element.21.sums_ref, f32[32,256]{1,0:T(8,128)} %get-tuple-element.22.pk_ref, f32[1,1024]{1,0:T(1,128)} %get-tuple-element.23.log_in, f32[32,1024]{1,0:T(8,128)} %copy.22.ctf_ref, bf16[256,1024]{1,0:T(8,128)(2,1)} %copy.21.rott_ref), custom_call_target="tpu_custom_call" | custom-call | tf_op jit(solution)/shard_map/last_stage/pallas_call | solution.py:612
  (1 shorter events, 0.0 us)

commit v5 on v4

--- a/solution.py
+++ b/solution.py
@@ -110,17 +110,16 @@
     kinds_ref[:, SLOTS : 2 * SLOTS] = jnp.full((GROUPS, SLOTS), -1, I32)
 
 
-def turn_pixels(part_ref, xs_ref, perm, begin, end):
-    def make_perm(i, _):
-        r = iota((64, PIX), 0)
-        c = iota((64, PIX), 1)
-        hit = c == (r * CYC + i)
+def make_perm(perm):
+    def cycle(i, _):
+        hit = iota((64, PIX), 1) == iota((64, PIX), 0) * CYC + i
         perm[pl.ds(pl.multiple_of(i * 64, 64), 64), :] = onehot(hit)
         return 0
 
-    if begin == 0:
-        lax.fori_loop(0, CYC, make_perm, 0)
-
+    lax.fori_loop(0, CYC, cycle, 0)
+
+
+def turn_pixels(part_ref, xs_ref, perm, begin, end):
     def turn_rows(i, _):
         y = mm(part_ref[pl.ds(pl.multiple_of(i * 128, 128), 128), :], perm[...])
         for j in range(8):
@@ -130,7 +129,7 @@
     lax.fori_loop(begin, end, turn_rows, 0)
 
 
-def start_kernel(cand_ref, kind_ref, mine_ref, part_ref, tab_ref, kinds_ref, rho_ref, pack_ref, all_ref, xs_ref, perm, send_sem, recv_sem, own_sem):
+def start_kernel(cand_ref, kind_ref, own_refs, part_ref, ctf_ref, tab_ref, kinds_ref, rho_ref, pack_ref, all_ref, xs_ref, ctf_out, perm, build, mine_ref, send_sem, recv_sem, own_sem):
     me = lax.axis_index("dom")
     row = lax.axis_index("cls")
     z, x, core = me // 8, (me // 2) % X, me % 2
@@ -145,6 +144,14 @@
     barrier = pltpu.get_barrier_semaphore()
     for n in range(11):
         pl.semaphore_signal(barrier, inc=1, device_id=(row, peer(n)), device_id_type=MESH)
+    refs = own_refs[...].astype(F32)
+    for c in range(CPG):
+        for l in range(CYC):
+            r = (c % 2) * CYC + l
+            build[r : r + 1, (c // 2) * ANG : (c // 2 + 1) * ANG] = refs[c : c + 1, l * ANG : (l + 1) * ANG]
+    mine_ref[...] = build[...].astype(BF16)
+    route(me, cand_ref, kind_ref, tab_ref, kinds_ref, rho_ref, pack_ref)
+    make_perm(perm)
     pl.semaphore_wait(barrier, 11)
 
     def copy(n):
@@ -170,21 +177,23 @@
         c.start()
     own = pltpu.make_async_copy(mine_ref, all_ref.at[z, x, core], own_sem)
     own.start()
-    route(me, cand_ref, kind_ref, tab_ref, kinds_ref, rho_ref, pack_ref)
+    y = mm(jnp.concatenate(list(pieces(ctf_ref[...])), axis=0), perm[...])
+    ctf_out[...] = y[0:KINDS] + y[KINDS : 2 * KINDS] + y[2 * KINDS : 3 * KINDS]
+    turn_pixels(part_ref, xs_ref, perm, 0, 4)
     own.wait()
     for c in first:
         c.wait()
     for c in second:
         c.start()
-    turn_pixels(part_ref, xs_ref, perm, 0, 4)
+    turn_pixels(part_ref, xs_ref, perm, 4, 7)
     for c in second:
         c.wait()
     third.start()
-    turn_pixels(part_ref, xs_ref, perm, 4, 8)
+    turn_pixels(part_ref, xs_ref, perm, 7, 8)
     third.wait()
 
 
-def start_stage(cand_t, kinds_row, mine, particles):
+def start_stage(cand_t, kinds_row, references, particles, ctf_table):
     return pl.pallas_call(
         start_kernel,
         out_shape=(
@@ -194,18 +203,21 @@
             jax.ShapeDtypeStruct((1, 384), I32),
             jax.ShapeDtypeStruct((Z, X, 2, 32, 128), BF16),
             jax.ShapeDtypeStruct((TOK * 8, 128), F32),
+            jax.ShapeDtypeStruct((KINDS, PIX), F32),
         ),
-        in_specs=vm(4),
-        out_specs=tuple(vm(6)),
+        in_specs=vm(5),
+        out_specs=tuple(vm(7)),
         scratch_shapes=[
             pltpu.VMEM((PIX, PIX), BF16),
+            pltpu.VMEM((32, 128), F32),
+            pltpu.VMEM((32, 128), BF16),
             pltpu.SemaphoreType.DMA((11,)),
             pltpu.SemaphoreType.DMA((11,)),
             pltpu.SemaphoreType.DMA,
         ],
         compiler_params=pltpu.CompilerParams(collective_id=0, has_side_effects=True, vmem_limit_bytes=VMEM_LIMIT),
         name="start_stage",
-    )(cand_t, kinds_row, mine, particles)
+    )(cand_t, kinds_row, references, particles, ctf_table)
 
 
 def turned(raw, rsq):
@@ -261,9 +273,10 @@
     )
 
 
-def main_kernel(tab_ref, pack_ref, xs, refs_ref, rott_ref, ctf_ref, kinds_ref, rho_ref, sums_ref, pk_ref, log_ref, cs, power, bd, raw, rot_a, rot_b, stage_a, stage_b, hits_a, hits_b, wall, table, packed, far, held, near, total_ref, w_ref, wide, stat, stat_recv, rsq_a, rsq_b, raw_a, raw_b, parts, msg, got, mine, others, ring, ring2, stat_sem, ssem, rsem, share_sem):
+def main_kernel(tab_ref, pack_ref, xs, refs_ref, rott_ref, ctf_ref, kinds_ref, rho_ref, sums_ref, pk_ref, log_ref, cs, power, bd, raw, rot_a, rot_b, stage_a, stage_b, hits_a, hits_b, weights_a, weights_b, wall, table, packed, far, held, near, total_ref, w_ref, wide, stat, stat_recv, rsq_a, rsq_b, raw_a, raw_b, parts, msg, got, mine, others, ring, ring2, stat_sem, ssem, rsem, share_sem):
     rots, stages, hits = (rot_a, rot_b), (stage_a, stage_b), (hits_a, hits_b)
     rsqs, raws = (rsq_a, rsq_b), (raw_a, raw_b)
+    weights = (weights_a, weights_b)
     me = lax.axis_index("cls")
     dom = lax.axis_index("dom")
     right, left, across = lax.rem(me + 1, SHARES), lax.rem(me + 3, SHARES), lax.rem(me + 2, SHARES)
@@ -355,6 +368,7 @@
         for j in range(8):
             col = stage[pl.ds(j, SLOTS, stride=8), :].astype(BF16)
             wall[g, :, j * 128 : (j + 1) * 128] = col
+            weights[u][:, j * 128 : (j + 1) * 128] = col
         kinds = kinds_ref[pl.ds(g, 1), :]
         hit = jnp.where(((k_row & 31) == kinds) & (k_row < 64), 1.0, 0.0)
         hits[u][...] = jnp.transpose(hit)[0:SLOTS, :].astype(BF16)
@@ -366,7 +380,7 @@
         for part in range(2):
             at = slice(part * 512, (part + 1) * 512)
             r = rot[at, :]
-            z = mm(wall[g, :, at], r)
+            z = mm(weights[u][:, at], r)
             y = mm(power[:, at], r * r)
             total = z if total is None else total + z
             en = y if en is None else en + y
@@ -649,6 +663,8 @@
             pltpu.VMEM((SLOTS * 8, 128), F32),
             pltpu.VMEM((SLOTS, 128), BF16),
             pltpu.VMEM((SLOTS, 128), BF16),
+            pltpu.VMEM((SLOTS, PIX), BF16),
+            pltpu.VMEM((SLOTS, PIX), BF16),
             pltpu.VMEM((GROUPS, SLOTS, PIX), BF16),
             pltpu.VMEM((GROUPS * 8, 8, PAIRS), F32),
             pltpu.VMEM((CHUNKS, SHARES, 64, PAIRS), F32),
@@ -681,16 +697,11 @@
     )(tab, packing, xs.reshape(TOK, 8, 128), refs.reshape(GROUPS, 32, 128), rott, ctf, kinds, rho)
 
 
-def prepared(candidates, defocus, ctf_table, references, rotations):
-    mine = references.reshape(2, 2, CYC, ANG).transpose(1, 2, 0, 3).reshape(32, 128)
+def local(particles, candidates, defocus, ctf_table, references, rotations):
     rott = rotations.reshape(ROT, CYC, 4 * ANG).transpose(2, 1, 0).reshape(256, 1024)
-    ctf = ctf_table.reshape(KINDS, CYC, ANG).transpose(0, 2, 1).reshape(KINDS, PIX)
-    return mine, rott, ctf, candidates.T, defocus.reshape(1, TOK)
-
-
-def local(particles, candidates, defocus, ctf_table, references, rotations):
-    mine, rott, ctf, cand_t, kinds_row = prepared(candidates, defocus, ctf_table, references, rotations)
-    tab, kinds, rho, packing, refs, xs = start_stage(cand_t, kinds_row, mine, particles)
+    tab, kinds, rho, packing, refs, xs, ctf = start_stage(
+        candidates.T, defocus.reshape(1, TOK), references, particles, ctf_table
+    )
     sums, pk, log = main_stage(tab, packing, xs, refs, rott, ctf, kinds, rho)
     cs, cw, log = last_stage(sums, pk, log, ctf, rott)
     return cs, cw, log.reshape(TOK)

time: 159 us -> 151 us (0.950)
  Pallas kernels: 151 us -> 146 us
  local copies, waits for them, and re-layouts: 6.71 us -> 3.1 us
    pallas_call x1, Pallas kernels: 124 us -> 119 us  [main_stage(): pl.pallas_call(main_kernel, out_shape=(jax.ShapeDtypeStruct((32, 128), F3...]
    reshape x8 -> x2, local copies, waits for them, and re-layouts: 6.55 us -> 2.94 us  [local(): rotations.reshape(ROT, CYC, 4 * ANG).transpose(2, 1, 0).reshape(256, 1024)]
where the time goes in v5:
time: 151 us; the launch traced here: 150 us
  Pallas kernels  146 us (97%)
  local copies, waits for them, and re-layouts  3.1 us (2%)
    pallas_call x1, Pallas kernels, main_stage(): pl.pallas_call(main_kernel, out_shape=(jax.ShapeDtypeStruct((32, 128), F3...  119 us
    pallas_call x1, Pallas kernels, start_stage(): pl.pallas_call(start_kernel, out_shape=(jax.ShapeDtypeStruct((GROUPS, 2 *...  23.5 us
    pallas_call x1, Pallas kernels, last_stage(): pl.pallas_call(last_kernel, out_shape=(jax.ShapeDtypeStruct((CPG, PIX), B...  3.63 us

profile of v5, /device:TPU:1, one launch (start us, length us, event | category | flops | bytes accessed | tf_op | source)
XLA Modules:
  0.0 150.2 jit_solution(11979982412812797906)
XLA Ops:
  0.6 1.9 %reshape.27 = bf16[64,16,256]{2,1,0:T(8,128)(2,1)S(1)} reshape(bf16[64,64,64]{2,1,0:T(8,128)(2,1)} %param.11) | data formatting | bytes 1048576 | tf_op jit(solution)/shard_map/reshape | solution.py:701
  2.6 0.2 copy.12
  2.7 1.0 copy.13.rott_ref
  3.7 23.5 %start_stage.1 = (s32[64,128]{1,0:T(8,128)}, s32[64,128]{1,0:T(8,128)}, s32[2,1024]{1,0:T(2,128)}, s32[1,384]{1,0:T(1,128)}, bf16[8,4,2,32,128]{4,3,2,1,0:T(8,12...) custom-call(s32[2,1024]{1,0:T(2,128)} %bitcast.11, s32[1,1024]{1,0:T(1,128)} %bitcast.12, bf16[4,1024]{1,0:T(4,128)(2,1)} %own_refs.1, ...), custom_call_target="tpu_custom_call" | custom-call | tf_op jit(solution)/shard_map/start_stage/pallas_call | solution.py:197
  27.3 119.2 %main_stage.1 = (f32[32,128]{1,0:T(8,128)}, f32[32,256]{1,0:T(8,128)}, f32[1,1024]{1,0:T(1,128)}) custom-call(s32[64,128]{1,0:T(8,128)} %get-tuple-element.16.tab_ref, s32[1,384]{1,0:T(1,128)} %get-tuple-element.17.pack_ref, f32[1024,8,128]{2,1,0:T(8,128)} %bitcast.7, bf16[64,32,128]{2,1,0:T(8,128)(2,1)} %bitcast.10, bf16[256,1024]{1,0:T(8,128)(2,1)} %copy.13.rott_ref, ...), custom_call_target="tpu_custom_call" | custom-call | tf_op jit(solution)/shard_map/main_stage/pallas_call | solution.py:646
  146.5 3.6 %last_stage.1 = (bf16[4,1024]{1,0:T(4,128)(2,1)}, f32[4,1024]{1,0:T(4,128)}, f32[8,128]{1,0:T(8,128)}) custom-call(f32[32,128]{1,0:T(8,128)} %get-tuple-element.23.sums_ref, f32[32,256]{1,0:T(8,128)} %get-tuple-element.24.pk_ref, f32[1,1024]{1,0:T(1,128)} %get-tuple-element.25.log_in, f32[32,1024]{1,0:T(8,128)} %get-tuple-element.20.ctf_ref, ...), custom_call_target="tpu_custom_call" | custom-call | tf_op jit(solution)/shard_map/last_stage/pallas_call | solution.py:626
